TPU v7x, 128 devices: a whole 4x4x4 slice. The times are simulated.
128 devices in a mesh: slab: 16 (over x_hi, z, core), col: 8 (over x_lo, y).
Axes of the slice: x: 4 (x_hi: 2, x_lo: 2; x = x_hi * 2 + x_lo), y: 4, z: 4, core: 2. Of those that a mesh axis runs over, the one named last changes fastest.
Arguments:
- sensitivity: bfloat16 [3, 512, 65536], P(None, 'col', 'slab'), may hold values from -0.03125 to 0.03125
- residual_force: bfloat16 [3, 65536], P(None, 'slab'), may hold values from -6 to 6
- moments: float32 [6, 64, 1024], P(None, 'slab'), as said below
- zone_label: int32 [64, 1024], P('slab'), may hold values from 0 to 511, as said below
- misfit: float32 [64, 1024], P('slab'), may hold values from 0.1 to 10
Outputs:
- hessian: float32 [512, 512], P('col', 'slab')
- gradient: float32 [512], replicated
- zone_misfit: float32 [512], replicated
Inputs may be any that keep to these rules, and one draw needn't show every extreme that they name: zone_label is the box of a 8 x 8 x 8 partition of the specimen that holds the element, the in-plane box borders displaced by at most one element; every zone occurs. `moments`: each element's moment matrix is symmetric with positive diagonal, and each diagonal entry exceeds the sum of the magnitudes of the others in its row.
All inputs are finite; a program needn't handle non-finite values.
Results may differ from a plain program's by a relative error of at most 0.0003.
Values may be sent and summed in bfloat16 or wider, within the bound.
A program may use at most 128 MiB of HBM per device.

v0:
```python
import jax
import jax.numpy as jnp
from jax import lax
from jax.sharding import PartitionSpec as P

GX = 64
GY = 16


third = 1.0 / 3.0
sixth = 1.0 / 6.0


def shifted(value, axis, by):
    count = lax.axis_size(axis)
    pairs = [(i, i + by) for i in range(count) if 0 <= i + by < count]
    return lax.ppermute(value, axis, pairs)


def mix_pair(first, second):
    return (third * first + sixth * second, sixth * first + third * second)


def shift_ahead(field, step, keep):
    moved = jnp.concatenate([field[..., step:], jnp.zeros_like(field[..., :step])], axis=-1)
    if keep is None:
        return moved
    return jnp.where(keep, moved, 0.0)


def shift_behind(field, step, keep):
    moved = jnp.concatenate([jnp.zeros_like(field[..., :step]), field[..., :-step]], axis=-1)
    if keep is None:
        return moved
    return jnp.where(keep, moved, 0.0)


def apply_moments(moments, field):
    comps = [moments[k][None, :] for k in range(6)]
    first, second, last = (field[0], field[1], field[2])
    out_x = comps[0] * first + comps[3] * second + comps[4] * last
    out_y = comps[3] * first + comps[1] * second + comps[5] * last
    out_z = comps[4] * first + comps[5] * second + comps[2] * last
    return jnp.stack([out_x, out_y, out_z])


def element_layer(lower, upper, moments):
    plane = lower.shape[-1]
    pos_y = jnp.arange(plane, dtype=jnp.int32) % GY
    not_last = pos_y != GY - 1
    not_first = pos_y != 0
    mixed_z = mix_pair(lower, upper)
    results = []
    for side_z in range(2):
        field = mixed_z[side_z]
        mixed_x = mix_pair(field, shift_ahead(field, GY, None))
        values = []
        for side_x in range(2):
            layer = mixed_x[side_x]
            mixed_y = mix_pair(layer, shift_ahead(layer, 1, not_last))
            values.append([apply_moments(moments, mixed_y[side_y]) for side_y in range(2)])
        total = values[0][0]
        total = total + shift_behind(values[1][0], GY, None)
        total = total + shift_behind(values[0][1], 1, not_first)
        total = total + shift_behind(shift_behind(values[1][1], 1, not_first), GY, None)
        results.append(total)
    return (results[0], results[1])


def on_device(sensitivity, residual_force, moments, zone_label, misfit):
    cols = sensitivity.shape[1]
    layers = moments.shape[1]
    plane_size = GX * GY
    n_slab = lax.axis_size("slab")
    n_col = lax.axis_size("col")
    width = cols * n_col
    field = sensitivity.reshape(3, cols, layers, plane_size)
    above = shifted(sensitivity[:, :, :plane_size], "slab", -1)
    levels = []
    carry = None
    first_lower = None
    for level in range(layers):
        lower = field[:, :, level].astype(jnp.float32)
        if level + 1 < layers:
            upper = field[:, :, level + 1].astype(jnp.float32)
        else:
            upper = above.astype(jnp.float32)
        to_lower, to_upper = element_layer(lower, upper, moments[:, level])
        if level == 0:
            first_lower = to_lower
        else:
            levels.append((carry + to_lower).astype(jnp.bfloat16))
        carry = to_upper
    from_below = shifted(carry.astype(jnp.bfloat16), "slab", 1).astype(carry.dtype)
    levels.insert(0, (from_below + first_lower).astype(jnp.bfloat16))
    image = jnp.stack(levels, axis=2).reshape(3, cols, layers * plane_size)
    panel_rows = lax.dot_general(
        image,
        lax.all_gather(sensitivity, "col", axis=1, tiled=True),
        (((0, 2), (0, 2)), ((), ())),
        preferred_element_type=jnp.float32,
    )
    hessian = lax.psum_scatter(panel_rows, "slab", scatter_dimension=1, tiled=True)
    grad_part = lax.dot_general(
        residual_force,
        sensitivity,
        (((0, 1), (0, 2)), ((), ())),
        preferred_element_type=jnp.float32,
    )
    grad_full = lax.dynamic_update_slice_in_dim(
        jnp.zeros((width,), jnp.float32), grad_part, lax.axis_index("col") * cols, 0
    )
    elements = layers * plane_size
    share = elements // n_col
    offset = lax.axis_index("col") * share
    zone_part = lax.dynamic_slice_in_dim(zone_label.reshape(elements), offset, share, 0)
    misfit_part = lax.dynamic_slice_in_dim(misfit.reshape(elements), offset, share, 0)
    onehot = (zone_part[:, None] == jnp.arange(width, dtype=jnp.int32)[None, :]).astype(jnp.float32)
    zone_part_sum = jnp.dot(misfit_part, onehot, precision=lax.Precision.HIGHEST)
    gradient, zone_sums = lax.psum((grad_full, zone_part_sum), ("slab", "col"))
    zone_misfit = zone_sums * (width / (elements * n_slab))
    return (hessian, gradient, zone_misfit)


def solution(mesh):
    in_specs = (
        P(None, "col", "slab"),
        P(None, "slab"),
        P(None, "slab", None),
        P("slab", None),
        P("slab", None),
    )
    out_specs = (P("col", "slab"), P(), P())
    return jax.shard_map(
        on_device, mesh=mesh, in_specs=in_specs, out_specs=out_specs, check_vma=False
    )
```

profile of v0, /device:TPU:6, one launch (start us, length us, event | category | flops | bytes accessed | tf_op | source)
XLA Modules:
  0.0 329.5 jit_solution(12702796365399645540)
XLA Ops:
  7.2 0.7 all-gather.2.cloned.1.call-update
  8.0 0.6 copy-done
  8.6 0.8 slice.768
  9.3 6.2 %collective-permute-start = (bf16[3,64,1024]{2,1,0:T(8,128)(2,1)}, bf16[3,64,1024]{2,1,0:T(8,128)(2,1)}, u32[]{:S(2)}, u32[]{:S(2)}) collective-permute-start(bf16[3,64,1024]{2,1,0:T(8,128)(2,1)} %slice.768), channel_id=1, source_target_pairs={{8,0},{16,8},{24,16},{32,24},{40,32},{48,40},{56,48},{64,56},{72,6... | collective-permute-start | bytes 1179656 | tf_op jit(solution)/shard_map/ppermute | solution.py:17
  15.6 1.2 reshape.1815
  16.8 3.2 fusion.94
  20.0 0.9 copy-done.1
  20.9 0.4 fusion.8
  21.3 0.9 copy-done.3
  22.1 1.2 slice.966
  23.5 0.5 convolution_bitcast_fusion.1
  24.0 0.5 fusion
  24.5 1.4 fusion.96
  25.9 1.2 fusion.14
  27.1 1.3 multiply_add_fusion.41
  28.4 0.6 fusion.92
  28.9 1.4 slice.1015
  30.3 2.3 slice.999
  32.7 1.2 slice.967
  33.9 1.2 slice.971
  35.2 155.7 %all-reduce.56 = (f32[512]{0:T(512)}, f32[512]{0:T(512)}) all-reduce(f32[512]{0:T(512)S(1)} %dynamic_update_slice.3, f32[512]{0:T(512)S(1)} %bitcast.370), channel_id=1, replica_groups=mesh['slab'=16,'col'=8] {'slab','col'}, use_global_device_ids=true, to_apply=%region_1.2 | all-reduce | flops 1024 | bytes 8192 | tf_op jit(solution)/shard_map/psum | solution.py:120
  190.9 0.6 fusion.91
  191.5 0.7 fusion.95
  192.2 1.5 fusion.3
  194.0 1.2 fusion.5
  195.6 2.6 multiply_add_fusion.45
  198.7 0.6 multiply_add_fusion.17
  199.3 1.2 slice.1048
  200.5 1.2 slice.1052
  201.7 1.2 slice.1064
  202.8 1.1 slice.1068
  204.0 1.2 slice.953
  205.4 0.3 multiply_add_fusion.35
  205.8 1.1 slice.983
  206.9 1.2 slice.987
  208.1 1.2 slice.1000
  209.3 1.2 slice.949
  210.4 1.2 slice.1004
  211.6 1.2 slice.1016
  212.8 1.2 slice.1020
  213.9 1.1 slice.1032
  215.1 1.2 slice.1036
  216.3 5.2 %multiply_add_fusion.42 = (f32[3,64,1024]{2,1,0:T(8,128)}, f32[3,64,1024]{2,1,0:T(8,128)}, f32[3,64,1024]{2,1,0:T(8,128)S(1)}, f32[3,64,1024]{2,1,0:T(8,128)S(1)...) fusion(f32[3,64,1024]{2,1,0:T(8,128)S(1)} %get-tuple-element.43, ...), kind=kLoop, calls=%fused_computation.212 | loop fusion | flops 8257536 | bytes 18870784 | tf_op jit(solution)/shard_map/add | solution.py:21
  221.5 2.1 multiply_add_fusion.122
  223.6 0.9 multiply_add_fusion.110
  224.6 5.7 %multiply_add_fusion.46 = (f32[3,64,1024]{2,1,0:T(8,128)}, f32[3,64,1024]{2,1,0:T(8,128)}, f32[3,64,1024]{2,1,0:T(8,128)}, f32[3,64,1024]{2,1,0:T(8,128)S(1)}, f...) fusion(f32[3,64,1024]{2,1,0:T(8,128)S(1)} %get-tuple-element.44, ...), kind=kLoop, calls=%fused_computation.217 | loop fusion | flops 8257536 | bytes 18870784 | tf_op jit(solution)/shard_map/add | solution.py:21
  230.4 1.3 multiply_add_fusion.98
  232.1 0.8 copy-done.10
  233.4 0.7 copy-done.9
  234.5 0.6 copy-done.20
  235.4 1.5 fusion.76
  237.0 0.7 fusion.81
  237.7 2.1 collective-permute-start.1
  239.8 1.0 multiply_add_fusion.10
  242.0 0.8 copy-done.5
  245.0 0.5 fusion.28
  245.5 1.4 fusion.87
  246.9 1.3 fusion.86
  248.2 1.3 fusion.85
  249.4 1.1 collective-permute-done.1
  250.5 0.7 fusion.84
  251.6 7.1 %convolution_bitcast_fusion = f32[64,512]{0,1:T(8,128)} fusion(bf16[3,64,4096]{2,1,0:T(8,128)(2,1)S(1)} %bitcast.171, bf16[3,512,4096]{2,1,0:T(8,128)(2,1)} %all-gather.2.cloned.1.call-done), kind=kOutput, calls=%fused_computation.1 | convolution fusion | flops 805306368 | bytes 14286848 | tf_op jit(solution)/shard_map/dot_general | solution.py:97
  258.7 0.6 broadcast_multiply_fusion
  259.3 63.4 %reduce-scatter.2.cloned.1.call-done = f32[64,32]{0,1:T(8,128)} async-done(((f32[64,512]{0,1:T(8,128)}), f32[64,32]{0,1:T(8,128)}) %reduce-scatter.2.cloned.1.call-update) | async-done | bytes 8208 | tf_op jit(solution)/shard_map/reduce_scatter | solution.py:103
  (144 shorter events, 6.9 us)
Async XLA Ops:
  7.2 1.4 copy-start
  7.2 244.4 %all-gather.2.cloned.1.call-start = ((), (), s32[]{:S(2)}) async-start(), calls=%async_computation.1 | async-start | bytes 14155776 | tf_op jit(solution)/shard_map/all_gather | solution.py:99
  7.9 314.8 %reduce-scatter.2.cloned.1.call-start = ((), (), s32[]{:S(2)}) async-start(), calls=%async_computation.2 | async-start | bytes 278528 | tf_op jit(solution)/shard_map/reduce_scatter | solution.py:103
  9.3 182.9 %collective-permute-start = (bf16[3,64,1024]{2,1,0:T(8,128)(2,1)}, bf16[3,64,1024]{2,1,0:T(8,128)(2,1)}, u32[]{:S(2)}, u32[]{:S(2)}) collective-permute-start(bf16[3,64,1024]{2,1,0:T(8,128)(2,1)} %slice.768), channel_id=1, source_target_pairs={{8,0},{16,8},{24,16},{32,24},{40,32},{48,40},{56,48},{64,56},{72,6... | collective-permute-start | bytes 1179656 | tf_op jit(solution)/shard_map/ppermute | solution.py:17
  20.0 0.9 copy-start.1
  20.9 2.4 copy-start.47
  20.9 2.4 copy-start.48
  20.9 2.6 copy-start.51
  21.3 0.9 copy-start.3
  22.1 3.8 %copy-start.19 = (bf16[3,64,1,1024]{3,2,1,0:T(2,128)(2,1)S(1)}, bf16[3,64,1,1024]{3,2,1,0:T(2,128)(2,1)}, u32[]{:S(2)}) copy-start(bf16[3,64,1,1024]{3,2,1,0:T(2,128)(2,1)} %get-tuple-element.57) | copy-start | bytes 1179652
  24.0 3.1 copy-start.4
  24.0 3.1 copy-start.18
  32.7 158.9 %copy-start.45 = (f32[6,4,1024]{2,1,0:T(4,128)S(1)}, f32[6,4,1024]{2,1,0:T(4,128)}, u32[]{:S(2)}) copy-start(f32[6,4,1024]{2,1,0:T(4,128)} %param.7) | copy-start | bytes 294916
  194.0 1.5 copy-start.2
  194.0 1.5 copy-start.17
  213.9 2.3 copy-start.49
  216.3 5.2 %copy-start.25 = (f32[1,1,1024]{2,1,0:T(1,128)S(1)}, f32[1,1,1024]{2,1,0:T(1,128)}, u32[]{:S(2)}) copy-start(f32[1,1,1024]{2,1,0:T(1,128)} %get-tuple-element.188) | copy-start | bytes 12292
  216.3 5.2 %copy-start.26 = (f32[1,1,1024]{2,1,0:T(1,128)S(1)}, f32[1,1,1024]{2,1,0:T(1,128)}, u32[]{:S(2)}) copy-start(f32[1,1,1024]{2,1,0:T(1,128)} %get-tuple-element.189) | copy-start | bytes 12292
  221.5 2.1 copy-start.11
  224.5 5.7 %copy-start.29 = (f32[1,1,1024]{2,1,0:T(1,128)S(1)}, f32[1,1,1024]{2,1,0:T(1,128)}, u32[]{:S(2)}) copy-start(f32[1,1,1024]{2,1,0:T(1,128)} %get-tuple-element.179) | copy-start | bytes 12292
  224.5 5.7 %copy-start.30 = (f32[1,1,1024]{2,1,0:T(1,128)S(1)}, f32[1,1,1024]{2,1,0:T(1,128)}, u32[]{:S(2)}) copy-start(f32[1,1,1024]{2,1,0:T(1,128)} %get-tuple-element.180) | copy-start | bytes 12292
  224.6 5.7 %copy-start.31 = (f32[1,1,1024]{2,1,0:T(1,128)S(1)}, f32[1,1,1024]{2,1,0:T(1,128)}, u32[]{:S(2)}) copy-start(f32[1,1,1024]{2,1,0:T(1,128)} %get-tuple-element.181) | copy-start | bytes 12292
  224.6 5.7 %copy-start.32 = (f32[1,1,1024]{2,1,0:T(1,128)S(1)}, f32[1,1,1024]{2,1,0:T(1,128)}, u32[]{:S(2)}) copy-start(f32[1,1,1024]{2,1,0:T(1,128)} %get-tuple-element.182) | copy-start | bytes 12292
  224.6 5.7 %copy-start.33 = (f32[1,1,1024]{2,1,0:T(1,128)S(1)}, f32[1,1,1024]{2,1,0:T(1,128)}, u32[]{:S(2)}) copy-start(f32[1,1,1024]{2,1,0:T(1,128)} %get-tuple-element.183) | copy-start | bytes 12292
  224.6 5.7 %copy-start.34 = (f32[1,1,1024]{2,1,0:T(1,128)S(1)}, f32[1,1,1024]{2,1,0:T(1,128)}, u32[]{:S(2)}) copy-start(f32[1,1,1024]{2,1,0:T(1,128)} %get-tuple-element.184) | copy-start | bytes 12292
  230.3 1.5 copy-start.12
  230.3 1.6 copy-start.7
  230.3 1.6 copy-start.35
  230.3 1.6 copy-start.36
  230.3 1.6 copy-start.37
  230.4 1.6 copy-start.42
  230.4 1.6 copy-start.43
  230.4 1.6 copy-start.44
  231.7 1.2 copy-start.10
  232.0 1.2 copy-start.6
  232.9 1.2 copy-start.9
  233.2 1.2 copy-start.8
  233.2 1.2 copy-start.27
  233.2 1.2 copy-start.28
  233.2 1.2 copy-start.38
  233.2 1.2 copy-start.39
  233.2 1.2 copy-start.40
  233.2 1.2 copy-start.41
  234.1 1.0 copy-start.20
  234.1 1.1 copy-start.21
  234.1 1.2 copy-start.22
  234.1 1.2 copy-start.23
  234.1 1.3 copy-start.24
  234.1 1.3 copy-start.46
  236.9 2.8 copy-start.13
  237.0 2.8 copy-start.14
  237.0 2.8 copy-start.15
  237.0 2.8 copy-start.16
  237.7 12.8 %collective-permute-start.1 = (bf16[3,64,1024]{2,1,0:T(8,128)(2,1)S(1)}, bf16[3,64,1024]{2,1,0:T(8,128)(2,1)S(1)}, u32[]{:S(2)}, u32[]{:S(2)}) collective-permute-start(bf16[3,64,1024]{2,1,0:T(8,128)(2,1)S(1)} %fusion.81), channel_id=1, source_target_pairs={{0,8},{8,16},{16,24},{24,32},{32,40},{40,48},{48,56},{56,64},{64,7... | collective-permute-start | bytes 1179656 | tf_op jit(solution)/shard_map/ppermute | solution.py:17
  241.7 1.1 copy-start.5
  251.6 7.1 %copy-start.50 = (f32[512]{0:T(512)S(1)}, f32[512]{0:T(512)}, u32[]{:S(2)}) copy-start(f32[512]{0:T(512)} %get-tuple-element.4) | copy-start | bytes 6148
Sparse Core Ops, SparseCore 0:
  9.6 133.5 all-gather.1
  258.9 63.7 reduce-scatter.1
where the time goes:
time: 331 us; the launch traced here: 330 us
  blocking collectives  156 us (47%)
  waiting for transfers between devices  65.2 us (20%)
  other arithmetic  38.8 us (12%)
  local copies, waits for them, and re-layouts  38.7 us (12%)
  between operations  14.8 us (4%)
  starting transfers between devices  8.34 us (3%)
  matrix products  8.09 us (2%)
    psum x1, blocking collectives, on_device(): gradient, zone_sums = lax.psum((grad_full, zone_part_sum), ('slab', 'col'))  156 us
    reduce_scatter x1, waiting for transfers between devices, on_device(): lax.psum_scatter(panel_rows, 'slab', scatter_dimension=1, tiled=True)  63.4 us
    slice x24, local copies, waits for them, and re-layouts, shift_ahead(): field[..., step:]  25 us
    add x11, other arithmetic, mix_pair(): return (third * first + sixth * second, sixth * first + third * second)  21 us
    add x32, other arithmetic, apply_moments(): out_x = comps[0] * first + comps[3] * second + comps[4] * last  8.5 us
    ppermute x2, starting transfers between devices, shifted(): return lax.ppermute(value, axis, pairs)  8.27 us
    dot_general x1, matrix products, on_device(): lax.dot_general(image, lax.all_gather(sensitivity, 'col', axis=1, tiled=T...  7.08 us
  transfers between devices with their start and end apart: 4, of which 2 were waited for; matrix products, arithmetic and copies ran while one was open for 22% of the time, Pallas kernels for 0%

commit v1 on v0

v1 whole, which is shorter than its diff:
```python
import functools

import jax
import jax.numpy as jnp
from jax import lax
from jax.experimental import pallas as pl
from jax.experimental.pallas import tpu as pltpu
from jax.sharding import PartitionSpec as P

MESH = pl.DeviceIdType.MESH
GX = 64
GY = 16
PLANE = GX * GY
LAYERS = 4
COLS = 64
WIDTH = 512
TILE = 128
KW = 768
ROWS = WIDTH + 16
BF = jnp.bfloat16
F32 = jnp.float32
NT = (((1,), (1,)), ((), ()))
OFFS = ((0, 1), (0, 3), (1, 0), (0, 2), (1, 1), (1, 3), (1, 2))


def iota(shape, dim):
    return lax.broadcasted_iota(jnp.int32, shape, dim)


def mix_weights():
    src = jnp.arange(2 * TILE, dtype=jnp.int32)[None, :, None]
    elem = jnp.arange(TILE, dtype=jnp.int32)[None, None, :]
    layer = jnp.arange(LAYERS + 1, dtype=jnp.int32)[:, None, None]
    ex, ey = elem // GY, elem % GY
    parts = []
    for b in range(2):
        for c in range(2):
            total = jnp.zeros((LAYERS + 1, 2 * TILE, TILE), F32)
            for b2 in range(2):
                for c2 in range(2):
                    weight = (2.0 if b == b2 else 1.0) * (2.0 if c == c2 else 1.0)
                    nx, ny = ex + b2, ey + c2
                    node = jnp.where(nx < 8, nx * GY + ny, TILE + layer * GY + ny)
                    total = total + jnp.where((src == node) & (ny < GY), weight, 0.0)
            parts.append(total)
    return jnp.concatenate(parts, axis=2).astype(BF)


def pick_weights():
    src = jnp.arange((LAYERS + 1) * TILE, dtype=jnp.int32)[:, None]
    dst = jnp.arange(TILE, dtype=jnp.int32)[None, :]
    return ((src // TILE == dst // GY) & (src % TILE == dst % GY)).astype(BF)


def kernel(
    s_any, res_ref, mom_ref, lab_ref, mis_ref, w_ref, pick_ref,
    h_out, e_out,
    sloc, zbuf, hal, sbuf, img, fbuf, gbuf, hacc, hrecv, erecv, hs, r1, m2, r2,
    loc_sem, z_sem, ss, rs, own_sem, p0_sem, s1, q1, s2, q2,
):
    s = lax.axis_index("slab")
    c = lax.axis_index("col")
    core = lax.rem(s, 2)
    z = lax.rem(s // 2, 4)
    xh = s // 8
    xl = c // 4
    y = lax.rem(c, 4)
    d = s // 2

    def col_peer(dx, dy):
        return lax.rem(xl + dx, 2) * 4 + lax.rem(y + dy + 4, 4)

    def slab_peer(dx, dz):
        return (lax.rem(xh + dx, 2) * 4 + lax.rem(z + dz + 4, 4)) * 2 + core

    partner = s + 1 - 2 * core
    bar = pltpu.get_barrier_semaphore()
    for dx, dy in OFFS:
        pl.semaphore_signal(bar, inc=1, device_id=(s, col_peer(dx, dy)), device_id_type=MESH)
        pl.semaphore_signal(bar, inc=1, device_id=(slab_peer(dx, dy), c), device_id_type=MESH)
    pl.semaphore_signal(bar, inc=1, device_id=(partner, c), device_id_type=MESH)
    pl.semaphore_signal(bar, inc=1, device_id=(lax.rem(s + 1, 16), c), device_id_type=MESH)
    pl.semaphore_signal(bar, inc=1, device_id=(lax.rem(s + 15, 16), c), device_id_type=MESH)
    load = pltpu.make_async_copy(s_any, sloc, loc_sem)
    load.start()

    def tile_at(ref, who, t):
        return ref.at[:, pl.ds(pl.multiple_of(who * COLS, COLS), COLS), pl.ds(t * TILE, TILE)]

    def lanes(l, who):
        return pl.ds(pl.multiple_of(l * PLANE + who * TILE, TILE), TILE)

    for l in range(LAYERS):
        pltpu.make_async_copy(s_any.at[:, :, lanes(l, c)], tile_at(sbuf, c, l), rs.at[c, l]).start()

    @pl.when(s == 15)
    def _():
        zbuf[...] = jnp.zeros_like(zbuf)

    pl.semaphore_wait(bar, 17)
    down = pltpu.make_async_remote_copy(
        src_ref=s_any.at[:, :, pl.ds(0, PLANE)], dst_ref=zbuf, send_sem=z_sem.at[0], recv_sem=z_sem.at[1],
        device_id=(lax.rem(s + 15, 16), c), device_id_type=MESH)

    @pl.when(s > 0)
    def _():
        down.start()

    def send(i, t):
        dx, dy = OFFS[i]
        who = col_peer(dx, dy)
        if t < LAYERS:
            src = s_any.at[:, :, lanes(t, who)]
        elif t == LAYERS:
            src = zbuf.at[:, :, lanes(0, who)]
        else:
            src = hal.at[who]
        return pltpu.make_async_remote_copy(
            src_ref=src, dst_ref=tile_at(sbuf, c, t), send_sem=ss.at[i, t], recv_sem=rs.at[c, t],
            device_id=(s, who), device_id_type=MESH)

    early = 3
    for i in range(early):
        for t in range(LAYERS):
            send(i, t).start()

    ctile = pl.ds(pl.multiple_of(c * TILE, TILE), TILE)
    for k in range(6):
        for l in range(LAYERS):
            gbuf[k, l] = jnp.broadcast_to(mom_ref[k, pl.ds(l, 1), ctile] * (1.0 / 216.0), (16, TILE))
    row16 = iota((16, TILE), 0)
    for k in range(3):
        for t in range(LAYERS + 2):
            if t < LAYERS:
                row = jnp.broadcast_to(res_ref[pl.ds(k, 1), lanes(t, c)].astype(F32), (16, TILE))
                val = jnp.where(row16 == 0, row, 0.0)
            else:
                val = jnp.zeros((16, TILE), F32)
            img[k, WIDTH:ROWS, t * TILE:(t + 1) * TILE] = val.astype(BF)
    parts = []
    for l in range(LAYERS):
        x = mis_ref[pl.ds(l, 1), ctile]
        hi = x.astype(BF).astype(F32)
        mid = (x - hi).astype(BF).astype(F32)
        lo = x - hi - mid
        full = jnp.where(row16 == 1, jnp.broadcast_to(hi, (16, TILE)), 0.0)
        full = jnp.where(row16 == 2, jnp.broadcast_to(mid, (16, TILE)), full)
        full = jnp.where(row16 == 3, jnp.broadcast_to(lo, (16, TILE)), full)
        parts.append(full.astype(BF))
    zone_lhs = jnp.concatenate(parts, axis=1)
    for half in range(2):
        row = iota((256, TILE), 0)
        zone_id = (row // 32) * 64 + half * 32 + lax.rem(row, 32)
        hot = jnp.concatenate([
            jnp.where(jnp.broadcast_to(lab_ref[pl.ds(l, 1), ctile], (256, TILE)) == zone_id, 1.0, 0.0).astype(BF)
            for l in range(LAYERS)], axis=1)
        hacc[half, WIDTH:ROWS, :] = lax.dot_general(zone_lhs, hot, NT, preferred_element_type=F32)

    load.wait()

    @pl.when(s < 15)
    def _():
        down.wait_recv()

    for who in range(8):
        if who == 7:
            hal[7] = jnp.zeros((3, COLS, TILE), BF)
        else:
            at = (who + 1) * TILE
            tiles = [sloc[:, :, l * PLANE + at:l * PLANE + at + TILE].reshape(3 * COLS, TILE) for l in range(LAYERS)]
            tiles.append(zbuf[:, :, at:at + TILE].reshape(3 * COLS, TILE))
            got = jnp.dot(jnp.concatenate(tiles, axis=1), pick_ref[...], preferred_element_type=F32)
            hal[who] = got.astype(BF).reshape(3, COLS, TILE)

    for i in range(early):
        for t in (LAYERS, LAYERS + 1):
            send(i, t).start()
    for i in range(early, 7):
        for t in range(LAYERS + 2):
            send(i, t).start()
    pltpu.make_async_copy(zbuf.at[:, :, lanes(0, c)], tile_at(sbuf, c, LAYERS), rs.at[c, LAYERS]).start()
    pltpu.make_async_copy(hal.at[c], tile_at(sbuf, c, LAYERS + 1), rs.at[c, LAYERS + 1]).start()

    lane = iota((16, TILE), 1)
    not_first = lax.rem(lane, GY) != 0
    inside = lane >= GY

    def block(src):
        for t in range(LAYERS + 2):
            at = tile_at(sbuf, src, t)
            pltpu.make_async_copy(at, at, rs.at[src, t]).wait()
        base = pl.multiple_of(src * COLS, COLS)
        halo = sbuf[:, pl.ds(base, COLS), KW - TILE:KW].reshape(3 * COLS, TILE)
        for l in range(LAYERS + 1):
            here = sbuf[:, pl.ds(base, COLS), l * TILE:(l + 1) * TILE].reshape(3 * COLS, TILE)
            both = jnp.concatenate([here, halo], axis=1)
            got = jnp.dot(both, w_ref[l], preferred_element_type=F32)
            fbuf[l] = got.reshape(3, COLS, 4 * TILE)

        @pl.loop(0, COLS // 16)
        def _(r):
            rows = pl.ds(pl.multiple_of(r * 16, 16), 16)
            dest = pl.ds(pl.multiple_of(base + r * 16, 16), 16)
            carry = [[None] * 3 for _ in range(4)]
            edge = [jnp.zeros((16, TILE), F32) for _ in range(3)]
            for n in range(LAYERS + 1):
                unit = [[None] * 3 for _ in range(4)]
                if n < LAYERS:
                    g = [gbuf[k, n] for k in range(6)]
                    for q in range(4):
                        low, high = [], []
                        for k in range(3):
                            first = fbuf[n, k, rows, q * TILE:(q + 1) * TILE]
                            second = fbuf[n + 1, k, rows, q * TILE:(q + 1) * TILE]
                            both = first + second
                            low.append(first + both)
                            high.append(second + both)

                        def apply(v):
                            return [
                                g[0] * v[0] + g[3] * v[1] + g[4] * v[2],
                                g[3] * v[0] + g[1] * v[1] + g[5] * v[2],
                                g[4] * v[0] + g[5] * v[1] + g[2] * v[2],
                            ]

                        low, high = apply(low), apply(high)
                        for k in range(3):
                            unit[q][k] = low[k] if n == 0 else carry[q][k] + low[k]
                            carry[q][k] = high[k]
                else:
                    unit = carry
                for k in range(3):
                    near = unit[0][k] + jnp.where(not_first, pltpu.roll(unit[1][k], 1, 1), 0.0)
                    far = unit[2][k] + jnp.where(not_first, pltpu.roll(unit[3][k], 1, 1), 0.0)
                    moved = pltpu.roll(far, GY, 1)
                    img[k, dest, n * TILE:(n + 1) * TILE] = (near + jnp.where(inside, moved, 0.0)).astype(BF)
                    if n > 0:
                        moved = pltpu.roll(far, GY * (n + 1), 1)
                    edge[k] = jnp.where((lane >= GY * n) & (lane < GY * (n + 1)), moved, edge[k])
            for k in range(3):
                img[k, dest, KW - TILE:KW] = edge[k].astype(BF)

    block(c)
    for dx, dy in OFFS:
        block(col_peer(dx, -dy))

    def panel(half):
        total = None
        for k in range(3):
            rhs = jnp.concatenate(
                [sbuf[k, pl.ds(pl.multiple_of(e * 64 + half * 32, 32), 32), :] for e in range(8)], axis=0)
            got = lax.dot_general(img[k], rhs, NT, preferred_element_type=F32)
            total = got if total is None else total + got
        hacc[half, 0:WIDTH, :] = total[:WIDTH]
        hacc[half, WIDTH:ROWS, :] = hacc[half, WIDTH:ROWS, :] + total[WIDTH:]

    other = 1 - core
    panel(other)
    swap = pltpu.make_async_remote_copy(
        src_ref=hacc.at[other], dst_ref=hrecv, send_sem=p0_sem.at[0], recv_sem=p0_sem.at[1],
        device_id=(partner, c), device_id_type=MESH)
    swap.start()
    panel(core)
    swap_e = pltpu.make_async_remote_copy(
        src_ref=hacc.at[core, pl.ds(WIDTH, 16), :], dst_ref=erecv, send_sem=p0_sem.at[2], recv_sem=p0_sem.at[3],
        device_id=(partner, c), device_id_type=MESH)
    swap_e.start()
    swap.wait_recv()
    swap_e.wait_recv()
    mine = hacc[core, WIDTH:WIDTH + 8, :] + hrecv[WIDTH:WIDTH + 8, :]
    theirs = hacc[other, WIDTH:WIDTH + 8, :] + erecv[0:8, :]
    even = jnp.where(core == 0, mine, theirs)
    odd = jnp.where(core == 0, theirs, mine)
    for who in range(8):
        hs[who, 0:COLS, :] = hacc[core, who * COLS:(who + 1) * COLS, :] + hrecv[who * COLS:(who + 1) * COLS, :]
        hs[who, COLS:COLS + 8, :] = even
        hs[who, COLS + 8:COLS + 16, :] = odd

    def send1(i):
        who = col_peer(*OFFS[i])
        return pltpu.make_async_remote_copy(
            src_ref=hs.at[who], dst_ref=r1.at[c], send_sem=s1.at[i], recv_sem=q1.at[c],
            device_id=(s, who), device_id_type=MESH)

    for i in range(7):
        send1(i).start()
    r1[c] = hs[c]
    for dx, dy in OFFS:
        who = col_peer(dx, -dy)
        pltpu.make_async_copy(r1.at[who], r1.at[who], q1.at[who]).wait()
    total = r1[0]
    for who in range(1, 8):
        total = total + r1[who]
    tail = total[COLS:COLS + 16]
    tail_rows = []
    for j in range(2):
        for half in range(2):
            for a in range(2):
                piece = tail[half * 8:half * 8 + 8, a * TILE:(a + 1) * TILE]
                if j == 0:
                    tail_rows.append(piece[0:1])
                else:
                    tail_rows.append(piece[1:2] + piece[2:3] + piece[3:4])
    ext = jnp.concatenate(tail_rows, axis=0)
    group = lane // 32
    for e in range(8):
        a, b = e // 4, e % 4
        packed = None
        for g in range(4):
            piece = total[16 * g:16 * g + 16, a * TILE:(a + 1) * TILE]
            shift = (32 * g - 32 * b) % TILE
            if shift:
                piece = pltpu.roll(piece, shift, 1)
            packed = piece if packed is None else jnp.where(group == g, piece, packed)
        m2[e, 0:16, :] = packed
        m2[e, 16:24, :] = ext

    def send2(i):
        to = slab_peer(*OFFS[i])
        return pltpu.make_async_remote_copy(
            src_ref=m2.at[to // 2], dst_ref=r2.at[d], send_sem=s2.at[i], recv_sem=q2.at[d],
            device_id=(to, c), device_id_type=MESH)

    for i in range(7):
        send2(i).start()
    r2[d] = m2[d]
    for dx, dz in OFFS:
        who = slab_peer(dx, -dz) // 2
        pltpu.make_async_copy(r2.at[who], r2.at[who], q2.at[who]).wait()
    total = r2[0]
    for who in range(1, 8):
        total = total + r2[who]
    for g in range(4):
        piece = total[0:16]
        if g:
            piece = pltpu.roll(piece, TILE - 32 * g, 1)
        h_out[16 * g:16 * g + 16, :] = piece[:, 0:32]
    ext = total[16:24]
    lane1 = iota((1, TILE), 1) // 32
    for j in range(2):
        for t in range(4):
            full = None
            for p in range(4):
                e, half = 2 * t + p // 2, p % 2
                row = j * 4 + half * 2 + e // 4
                piece = ext[row:row + 1]
                shift = (32 * p - 32 * (e % 4)) % TILE
                if shift:
                    piece = pltpu.roll(piece, shift, 1)
                full = piece if full is None else jnp.where(lane1 == p, piece, full)
            if j == 1:
                full = full * (WIDTH / 65536)
            e_out[4 * j + t:4 * j + t + 1, :] = full

    @pl.when(s > 0)
    def _():
        down.wait_send()

    for i in range(7):
        for t in range(LAYERS + 2):
            send(i, t).wait_send()
        send1(i).wait_send()
        send2(i).wait_send()
    swap.wait_send()
    swap_e.wait_send()


def on_device(sensitivity, residual_force, moments, zone_label, misfit):
    any_spec = pl.BlockSpec(memory_space=pl.ANY)
    vmem = pl.BlockSpec(memory_space=pltpu.VMEM)
    dma = pltpu.SemaphoreType.DMA
    h, e = pl.pallas_call(
        kernel,
        name="gauss_newton",
        out_shape=(jax.ShapeDtypeStruct((COLS, 32), F32), jax.ShapeDtypeStruct((8, TILE), F32)),
        in_specs=[any_spec] + [vmem] * 6,
        out_specs=(vmem, vmem),
        scratch_shapes=[
            pltpu.VMEM((3, COLS, LAYERS * PLANE), BF),
            pltpu.VMEM((3, COLS, PLANE), BF),
            pltpu.VMEM((8, 3, COLS, TILE), BF),
            pltpu.VMEM((3, WIDTH, KW), BF),
            pltpu.VMEM((3, ROWS, KW), BF),
            pltpu.VMEM((LAYERS + 1, 3, COLS, 4 * TILE), F32),
            pltpu.VMEM((6, LAYERS, 16, TILE), F32),
            pltpu.VMEM((2, ROWS, 256), F32),
            pltpu.VMEM((ROWS, 256), F32),
            pltpu.VMEM((16, 256), F32),
            pltpu.VMEM((8, COLS + 16, 256), F32),
            pltpu.VMEM((8, COLS + 16, 256), F32),
            pltpu.VMEM((8, 24, TILE), F32),
            pltpu.VMEM((8, 24, TILE), F32),
            dma(()), dma((2,)), dma((7, 6)), dma((8, 6)), dma(()), dma((4,)),
            dma((7,)), dma((8,)), dma((7,)), dma((8,)),
        ],
        compiler_params=pltpu.CompilerParams(collective_id=0, has_side_effects=True, vmem_limit_bytes=48 * 2**20),
    )(sensitivity, residual_force, moments, zone_label, misfit, mix_weights(), pick_weights())
    return h, e[0:4].reshape(WIDTH), e[4:8].reshape(WIDTH)


def solution(mesh):
    in_specs = (
        P(None, "col", "slab"),
        P(None, "slab"),
        P(None, "slab", None),
        P("slab", None),
        P("slab", None),
    )
    out_specs = (P("col", "slab"), P(), P())
    return jax.shard_map(
        on_device, mesh=mesh, in_specs=in_specs, out_specs=out_specs, check_vma=False
    )
```

time: 331 us -> 67.2 us (0.20)
  blocking collectives: 156 us -> 0 us
  waiting for transfers between devices: 65.2 us -> 0 us
  Pallas kernels: 0 us -> 62.6 us
  other arithmetic: 38.8 us -> 1.46 us
  local copies, waits for them, and re-layouts: 38.7 us -> 2.21 us
  between operations: 14.8 us -> 0.74 us
  starting transfers between devices: 8.34 us -> 0 us
  matrix products: 8.09 us -> 0 us
    psum x1 -> x0, blocking collectives: 156 us -> none  [on_device(): gradient, zone_sums = lax.psum((grad_full, zone_part_sum), ('slab', 'col'))]
    reduce_scatter x1 -> x0, waiting for transfers between devices: 63.4 us -> none  [on_device(): lax.psum_scatter(panel_rows, 'slab', scatter_dimension=1, tiled=True)]
    pallas_call x0 -> x1, Pallas kernels: none -> 62.6 us  [on_device(): pl.pallas_call(kernel, name='gauss_newton', out_shape=(jax.ShapeDtypeStru...]
    slice x28 -> x0, local copies, waits for them, and re-layouts: 31 us -> none  [the longest x24 25 us: shift_ahead(): field[..., step:]]
    add x43 -> x3, other arithmetic: 29.5 us -> 0.02 us  [mix_weights(): node = jnp.where(nx < 8, nx * GY + ny, TILE + layer * GY + ny)]
    ppermute x2 -> x0, starting transfers between devices: 8.27 us -> none  [shifted(): return lax.ppermute(value, axis, pairs)]
    dot_general x3 -> x0, matrix products: 8.09 us -> none  [the longest x1 7.08 us: on_device(): lax.dot_general(image, lax.all_gather(sensitivity, 'col', axis=1, tiled=T...]
    unnamed x106 -> x11, local copies, waits for them, and re-layouts: 5.99 us -> 1.63 us
  transfers between devices with their start and end apart: 4 -> 0, of which waited for: 2 -> 0; matrix products, arithmetic and copies ran while one was open for 22% -> 0% of each run, Pallas kernels for 0% -> 0%
where the time goes in v1:
time: 67.2 us; the launch traced here: 67 us
  Pallas kernels  62.6 us (93%)
  local copies, waits for them, and re-layouts  2.21 us (3%)
  other arithmetic  1.46 us (2%)
  between operations  0.74 us (1%)
    pallas_call x1, Pallas kernels, on_device(): pl.pallas_call(kernel, name='gauss_newton', out_shape=(jax.ShapeDtypeStru...  62.6 us
    unnamed x11, local copies, waits for them, and re-layouts  1.63 us

profile of v1, /device:TPU:6, one launch (start us, length us, event | category | flops | bytes accessed | tf_op | source)
XLA Modules:
  0.0 67.0 jit_solution(8256676862381766678)
XLA Ops:
  0.7 0.1 add_select_fusion.4
  0.8 0.9 %fusion.1 = (bf16[5,256,128]{2,1,0:T(8,128)(2,1)S(1)}, bf16[5,256,128]{2,1,0:T(8,128)(2,1)S(1)}, bf16[5,256,128]{2,1,0:T(8,128)(2,1)S(1)}, bf16[5,256,128]{2,1,0:T(8,128)(2,1)S(1)}) fusion(s32[5,128]{1,0:T(8,128)S(1)} %get-tuple-element.18, s32[5,128]{1,0:T(8,128)S(1)} %get-tuple-element.19, s32[5,128]{1,0:T(8,128)S(1)} %get-tuple-element.17, ...), kind=kLoop, calls=%fused_computation.14 | loop fusion | flops 5898240 | bytes 1321216 | tf_op jit(solution)/shard_map/convert
  1.7 0.0 copy-start
  1.7 0.0 copy-start.1
  1.7 0.0 copy-start.2
  1.8 0.0 copy-start.3
  1.8 0.0 copy-start.4
  1.8 0.2 pad_maximum_fusion.w_ref
  2.0 0.2 and_convert_fusion.pick_ref
  2.2 0.9 %copy-done = bf16[3,64,4096]{2,1,0:T(8,128)(2,1)S(1)} copy-done((bf16[3,64,4096]{2,1,0:T(8,128)(2,1)S(1)}, bf16[3,64,4096]{2,1,0:T(8,128)(2,1)}, u32[]{:S(2)}) %copy-start) | copy-done | bytes 1572888
  3.1 0.0 copy-done.1
  3.1 0.0 copy-done.2
  3.1 0.0 copy-done.3
  3.1 0.0 copy-done.4
  3.1 62.6 %gauss_newton.1 = (f32[64,32]{1,0:T(8,128)S(1)}, f32[8,128]{1,0:T(8,128)S(1)}) custom-call(bf16[3,64,4096]{2,1,0:T(8,128)(2,1)S(1)} %copy-done, bf16[3,4096]{1,0:T(4,128)(2,1)S(1)} %copy-done.2, f32[6,4,1024]{2,1,0:T(4,128)S(1)} %copy-done.1, s32[4,1024]{1,0:T(4,128)S(1)} %copy-done.3, f32[4,1024]{1,0:T(4,128)S(1)} %copy-done.4, ...), custom_call_target="tpu_custom_call" | custom-call | tf_op jit(solution)/shard_map/gauss_newton/pallas_call | solution.py:372
  65.7 0.7 %copy.8 = f32[64,32]{0,1:T(8,128)} copy(f32[64,32]{1,0:T(8,128)S(1)} %get-tuple-element.7) | data formatting | bytes 16384
  66.4 0.6 slice_bitcast_fusion
  (8 shorter events, 0.0 us)
Async XLA Ops:
  1.7 1.4 %copy-start = (bf16[3,64,4096]{2,1,0:T(8,128)(2,1)S(1)}, bf16[3,64,4096]{2,1,0:T(8,128)(2,1)}, u32[]{:S(2)}) copy-start(bf16[3,64,4096]{2,1,0:T(8,128)(2,1)} %s_any.1) | copy-start | bytes 4718596
  1.7 1.4 %copy-start.1 = (f32[6,4,1024]{2,1,0:T(4,128)S(1)}, f32[6,4,1024]{2,1,0:T(4,128)}, u32[]{:S(2)}) copy-start(f32[6,4,1024]{2,1,0:T(4,128)} %mom_ref.1) | copy-start | bytes 294916
  1.7 1.4 %copy-start.2 = (bf16[3,4096]{1,0:T(4,128)(2,1)S(1)}, bf16[3,4096]{1,0:T(4,128)(2,1)}, u32[]{:S(2)}) copy-start(bf16[3,4096]{1,0:T(4,128)(2,1)} %res_ref.1) | copy-start | bytes 73732
  1.8 1.4 %copy-start.3 = (s32[4,1024]{1,0:T(4,128)S(1)}, s32[4,1024]{1,0:T(4,128)}, u32[]{:S(2)}) copy-start(s32[4,1024]{1,0:T(4,128)} %lab_ref.1) | copy-start | bytes 49156
  1.8 1.4 %copy-start.4 = (f32[4,1024]{1,0:T(4,128)S(1)}, f32[4,1024]{1,0:T(4,128)}, u32[]{:S(2)}) copy-start(f32[4,1024]{1,0:T(4,128)} %mis_ref.1) | copy-start | bytes 49156

commit v2 on v1

v2 whole, which is shorter than its diff:
```python
import jax
import jax.numpy as jnp
from jax import lax
from jax.experimental import pallas as pl
from jax.experimental.pallas import tpu as pltpu
from jax.sharding import PartitionSpec as P

MESH = pl.DeviceIdType.MESH
GX = 64
GY = 16
PLANE = GX * GY
LAYERS = 4
COLS = 64
WIDTH = 512
TILE = 128
KW = 768
EDGE = 3 * 32
PART = 3 * COLS
CHUNK = EDGE + LAYERS * PART
BF = jnp.bfloat16
F32 = jnp.float32
NT = (((1,), (1,)), ((), ()))
OFFS = ((0, 1), (0, 3), (1, 0), (0, 2), (1, 1), (1, 3), (1, 2))


def iota(shape, dim):
    return lax.broadcasted_iota(jnp.int32, shape, dim)


def pair_weight(shift, side):
    return jnp.where(shift == side, 2.0, jnp.where(shift == 1 - side, 1.0, 0.0))


def fill_weights(w_ref, pick_ref):
    src, elem = iota((TILE, TILE), 0), iota((TILE, TILE), 1)
    ex, ey = elem // GY, lax.rem(elem, GY)
    sx, sy = src // GY, lax.rem(src, GY)
    for b in range(2):
        for c in range(2):
            wy = pair_weight(sy - ey, c)
            at = (2 * b + c) * TILE
            near = (pair_weight(sx - ex, b) * wy).astype(BF)
            far = pair_weight(8 - ex, b) * wy
            for l in range(LAYERS + 1):
                w_ref[l, 0:TILE, at:at + TILE] = near
                w_ref[l, TILE:2 * TILE, at:at + TILE] = jnp.where(sx == l, far, 0.0).astype(BF)
    for h in range(2):
        for l in range(LAYERS):
            hit = (src == elem - 64 * h - GY * l) & (src < GY)
            at = (h * LAYERS + l) * TILE
            pick_ref[at:at + TILE, :] = jnp.where(hit, 1.0, 0.0).astype(BF)


def kernel(
    s_any, res_any, mom_any, lab_any, mis_any,
    h_out, g_out, z_out,
    w_ref, pick_ref, res_ref, mom_ref, lab_ref, mis_ref,
    stage, chunk, above, edges, img, fbuf, gbuf, hacc, hrecv, pack, parts,
    esrc, e0, e1, e2,
    in_sem, st_sem, ss, rs, fs, fz, p0_sem, es, er, msem, rsem,
):
    s = lax.axis_index("slab")
    c = lax.axis_index("col")
    core = lax.rem(s, 2)
    z = lax.rem(s // 2, 4)
    xh = s // 8
    xl = c // 4
    y = lax.rem(c, 4)
    d = s // 2

    def col_peer(dx, dy):
        return lax.rem(xl + dx, 2) * 4 + lax.rem(y + dy + 4, 4)

    def slab_peer(dx, dz):
        return (lax.rem(xh + dx, 2) * 4 + lax.rem(z + dz + 4, 4)) * 2 + core

    order = [c] + [col_peer(dx, -dy) for dx, dy in OFFS]
    partner = s + 1 - 2 * core
    below = lax.rem(s + 15, 16)
    bar = pltpu.get_barrier_semaphore()
    for k in range(1, 64):
        to_c = lax.rem(c + k // 8, 8)
        to_d = lax.rem(d + k, 8)
        pl.semaphore_signal(bar, inc=1, device_id=(to_d * 2 + core, to_c), device_id_type=MESH)
    for to in (partner, lax.rem(s + 1, 16), below):
        pl.semaphore_signal(bar, inc=1, device_id=(to, c), device_id_type=MESH)

    def lanes(l, who):
        return pl.ds(pl.multiple_of(l * PLANE + who * TILE, TILE), TILE)

    for who in range(8):
        for l in range(LAYERS):
            for k in range(3):
                at = EDGE + l * PART + k * COLS
                pltpu.make_async_copy(
                    s_any.at[k, :, lanes(l, who)], stage.at[who, pl.ds(at, COLS), :], st_sem.at[who]).start()
    loads = [
        pltpu.make_async_copy(a, b, in_sem.at[i])
        for i, (a, b) in enumerate(((res_any, res_ref), (mom_any, mom_ref), (lab_any, lab_ref), (mis_any, mis_ref)))]
    for load in loads:
        load.start()

    @pl.when(s == 15)
    def _():
        above[...] = jnp.zeros_like(above)

    fill_weights(w_ref, pick_ref)
    for who in range(8):
        at = stage.at[who, pl.ds(EDGE, LAYERS * PART), :]
        pltpu.make_async_copy(at, at, st_sem.at[who]).wait()

    for who in range(8):
        if who == 7:
            stage[7, 0:EDGE, :] = jnp.zeros((EDGE, TILE), BF)
        else:
            tiles = [
                jnp.concatenate([
                    stage[who + 1, EDGE + l * PART + k * COLS + 32 * h:EDGE + l * PART + k * COLS + 32 * h + 32, :]
                    for k in range(3)], axis=0)
                for h in range(2) for l in range(LAYERS)]
            got = jnp.dot(jnp.concatenate(tiles, axis=1), pick_ref[...], preferred_element_type=F32)
            stage[who, 0:EDGE, :] = got.astype(BF)
    pltpu.make_async_copy(stage.at[c], chunk.at[c], rs.at[c]).start()

    pl.semaphore_wait(bar, 66)

    def send(i):
        who = col_peer(*OFFS[i])
        return pltpu.make_async_remote_copy(
            src_ref=stage.at[who], dst_ref=chunk.at[c], send_sem=ss.at[i], recv_sem=rs.at[c],
            device_id=(s, who), device_id_type=MESH)

    for i in range(7):
        send(i).start()

    for load in loads:
        load.wait()
    ctile = pl.ds(pl.multiple_of(c * TILE, TILE), TILE)
    for k in range(6):
        for l in range(LAYERS):
            gbuf[k, l] = jnp.broadcast_to(mom_ref[k, pl.ds(l, 1), ctile] * (1.0 / 216.0), (16, TILE))
    grad = None
    for k in range(3):
        for l in range(LAYERS):
            at = EDGE + l * PART + k * COLS
            rhs = jnp.concatenate([stage[who, at:at + COLS, :] for who in range(8)], axis=1)
            row = res_ref[k:k + 1, l * PLANE:(l + 1) * PLANE].astype(F32)
            lhs = jnp.broadcast_to(row, (16, PLANE)).astype(BF)
            got = lax.dot_general(lhs, rhs, NT, preferred_element_type=F32)
            grad = got if grad is None else grad + got
    row16 = iota((16, TILE), 0)
    pieces = []
    for l in range(LAYERS):
        x = mis_ref[pl.ds(l, 1), ctile]
        hi = x.astype(BF).astype(F32)
        mid = (x - hi).astype(BF).astype(F32)
        lo = x - hi - mid
        full = jnp.where(row16 == 0, jnp.broadcast_to(hi, (16, TILE)), 0.0)
        full = jnp.where(row16 == 1, jnp.broadcast_to(mid, (16, TILE)), full)
        full = jnp.where(row16 == 2, jnp.broadcast_to(lo, (16, TILE)), full)
        pieces.append(full.astype(BF))
    zone_lhs = jnp.concatenate(pieces, axis=1)
    esrc[0] = jnp.zeros((8, TILE), F32)
    esrc[0, 0:1, 0:COLS] = grad[0:1]
    for half in range(2):
        zone_id = iota((256, TILE), 0) + 256 * half
        hot = jnp.concatenate([
            jnp.where(jnp.broadcast_to(lab_ref[pl.ds(l, 1), ctile], (256, TILE)) == zone_id, 1.0, 0.0).astype(BF)
            for l in range(LAYERS)], axis=1)
        got = lax.dot_general(zone_lhs, hot, NT, preferred_element_type=F32)
        got = got[0:1] + got[1:2] + got[2:3]
        esrc[0, 4 + 2 * half:5 + 2 * half, :] = got[:, 0:TILE]
        esrc[0, 5 + 2 * half:6 + 2 * half, :] = got[:, TILE:2 * TILE]

    small0 = pltpu.make_async_remote_copy(
        src_ref=esrc.at[0], dst_ref=e0, send_sem=es.at[0], recv_sem=er.at[0],
        device_id=(partner, c), device_id_type=MESH)

    def small1(i):
        return pltpu.make_async_remote_copy(
            src_ref=esrc.at[1], dst_ref=e1.at[d], send_sem=es.at[1], recv_sem=er.at[1],
            device_id=(slab_peer(*OFFS[i]), c), device_id_type=MESH)

    def small2(i):
        return pltpu.make_async_remote_copy(
            src_ref=esrc.at[2], dst_ref=e2.at[c], send_sem=es.at[2], recv_sem=er.at[2],
            device_id=(s, col_peer(*OFFS[i])), device_id_type=MESH)

    def wait_all(ref, sem):
        pltpu.make_async_copy(ref, ref, sem).wait()

    small0.start()

    lane = iota((16, TILE), 1)
    not_first = lax.rem(lane, GY) != 0
    inside = lane >= GY
    edge_lane = iota((32, TILE), 1)

    def arrive(j):
        src = order[j]
        wait_all(chunk.at[src], rs.at[src])

        @pl.when(s > 0)
        def _():
            forward(j).start()

    def forward(j):
        src = order[j]
        return pltpu.make_async_remote_copy(
            src_ref=chunk.at[src, pl.ds(0, EDGE + PART), :], dst_ref=above.at[src],
            send_sem=fs.at[j], recv_sem=fz.at[src], device_id=(below, c), device_id_type=MESH)

    def block(j):
        src = order[j]

        @pl.when(s < 15)
        def _():
            wait_all(above.at[src], fz.at[src])

        for k in range(3):
            low = chunk[src, 32 * k:32 * k + 32, :].astype(F32)
            top = above[src, 32 * k:32 * k + 32, :].astype(F32)
            for h in range(2):
                first = low if h == 0 else pltpu.roll(low, 64, 1)
                second = top if h == 1 else pltpu.roll(top, 64, 1)
                both = jnp.where(edge_lane < 64, first, jnp.where(edge_lane < 80, second, 0.0))
                edges[src, COLS * k + 32 * h:COLS * k + 32 * h + 32, :] = both.astype(BF)
        halo = edges[src]
        for l in range(LAYERS + 1):
            if l < LAYERS:
                here = chunk[src, EDGE + l * PART:EDGE + (l + 1) * PART, :]
            else:
                here = above[src, EDGE:EDGE + PART, :]
            got = jnp.dot(jnp.concatenate([here, halo], axis=1), w_ref[l], preferred_element_type=F32)
            fbuf[l] = got.reshape(3, COLS, 4 * TILE)

        @pl.loop(0, COLS // 16)
        def _(r):
            rows = pl.ds(pl.multiple_of(r * 16, 16), 16)
            dest = pl.ds(pl.multiple_of(src * COLS + r * 16, 16), 16)
            carry = [[None] * 3 for _ in range(4)]
            edge = [jnp.zeros((16, TILE), F32) for _ in range(3)]
            for n in range(LAYERS + 1):
                unit = [[None] * 3 for _ in range(4)]
                if n < LAYERS:
                    g = [gbuf[k, n] for k in range(6)]
                    for q in range(4):
                        low, high = [], []
                        for k in range(3):
                            first = fbuf[n, k, rows, q * TILE:(q + 1) * TILE]
                            second = fbuf[n + 1, k, rows, q * TILE:(q + 1) * TILE]
                            both = first + second
                            low.append(first + both)
                            high.append(second + both)

                        def apply(v):
                            return [
                                g[0] * v[0] + g[3] * v[1] + g[4] * v[2],
                                g[3] * v[0] + g[1] * v[1] + g[5] * v[2],
                                g[4] * v[0] + g[5] * v[1] + g[2] * v[2],
                            ]

                        low, high = apply(low), apply(high)
                        for k in range(3):
                            unit[q][k] = low[k] if n == 0 else carry[q][k] + low[k]
                            carry[q][k] = high[k]
                else:
                    unit = carry
                for k in range(3):
                    near = unit[0][k] + jnp.where(not_first, pltpu.roll(unit[1][k], 1, 1), 0.0)
                    far = unit[2][k] + jnp.where(not_first, pltpu.roll(unit[3][k], 1, 1), 0.0)
                    moved = pltpu.roll(far, GY, 1)
                    img[k, dest, n * TILE:(n + 1) * TILE] = (near + jnp.where(inside, moved, 0.0)).astype(BF)
                    if n > 0:
                        moved = pltpu.roll(far, GY * (n + 1), 1)
                    edge[k] = jnp.where((lane >= GY * n) & (lane < GY * (n + 1)), moved, edge[k])
            for k in range(3):
                img[k, dest, KW - TILE:KW] = edge[k].astype(BF)

    arrive(0)
    for j in range(8):
        if j < 7:
            arrive(j + 1)
        block(j)
        if j == 1:
            small0.wait_recv()
            esrc[1] = esrc[0] + e0[...]
            for i in range(7):
                small1(i).start()
            e1[d] = esrc[1]
        if j == 4:
            wait_all(e1.at[pl.ds(0, 7)], er.at[1])
            total = e1[0]
            for who in range(1, 8):
                total = total + e1[who]
            esrc[2] = total
            for i in range(7):
                small2(i).start()
            e2[c] = total

    def panel(half):
        total = None
        for k in range(3):
            rhs = []
            for e in range(8):
                rows = pl.ds(pl.multiple_of(EDGE + k * COLS + half * 32, 32), 32)
                tiles = [
                    chunk[e, pl.ds(pl.multiple_of(EDGE + l * PART + k * COLS + half * 32, 32), 32), :]
                    for l in range(LAYERS)]
                tiles.append(above[e, rows, :])
                tiles.append(edges[e, pl.ds(pl.multiple_of(k * COLS + half * 32, 32), 32), :])
                rhs.append(jnp.concatenate(tiles, axis=1))
            got = lax.dot_general(img[k], jnp.concatenate(rhs, axis=0), NT, preferred_element_type=F32)
            total = got if total is None else total + got
        hacc[half] = total

    other = 1 - core
    panel(other)
    swap = pltpu.make_async_remote_copy(
        src_ref=hacc.at[other], dst_ref=hrecv, send_sem=p0_sem.at[0], recv_sem=p0_sem.at[1],
        device_id=(partner, c), device_id_type=MESH)
    swap.start()
    panel(core)
    swap.wait_recv()

    me = c * 8 + d
    group = lane // 32
    for i in range(8):
        to_c = lax.rem(c + i, 8)
        sums = []
        for g in range(4):
            rows = pl.ds(pl.multiple_of(to_c * COLS + 16 * g, 16), 16)
            sums.append(hacc[core, rows, :] + hrecv[rows, :])
        for e in range(8):
            a, b = e // 4, e % 4
            packed = None
            for g in range(4):
                piece = sums[g][:, a * TILE:(a + 1) * TILE]
                shift = (32 * g - 32 * b) % TILE
                if shift:
                    piece = pltpu.roll(piece, shift, 1)
                packed = piece if packed is None else jnp.where(group == g, piece, packed)
            pack[to_c * 8 + e] = packed
        for j in range(8):
            if i + j == 0:
                continue
            to_d = lax.rem(d + j, 8)
            pltpu.make_async_remote_copy(
                src_ref=pack.at[to_c * 8 + to_d], dst_ref=parts.at[me], send_sem=msem, recv_sem=rsem,
                device_id=(to_d * 2 + core, to_c), device_id_type=MESH).start()
    parts[me] = pack[me]

    wait_all(e2.at[pl.ds(0, 7)], er.at[2])
    zone = e2[0]
    for who in range(1, 8):
        zone = zone + e2[who]
    z_out[...] = zone[4:8] * (WIDTH / 65536)
    left = iota((1, TILE), 1) < COLS
    for t in range(4):
        g_out[t:t + 1, :] = jnp.where(left, e2[2 * t, 0:1, :], pltpu.roll(e2[2 * t + 1, 0:1, :], COLS, 1))

    wait_all(parts.at[pl.ds(0, 63)], rsem)
    total = parts[0]
    for who in range(1, 64):
        total = total + parts[who]
    rows = [pltpu.roll(total, TILE - 32 * g, 1) if g else total for g in range(4)]
    h_out[...] = jnp.transpose(jnp.concatenate(rows, axis=0))[0:32, :]

    @pl.when(s > 0)
    def _():
        for j in range(8):
            forward(j).wait_send()

    for i in range(7):
        send(i).wait_send()
    small0.wait_send()
    wait_all(e1.at[pl.ds(0, 7)], es.at[1])
    wait_all(e2.at[pl.ds(0, 7)], es.at[2])
    swap.wait_send()
    wait_all(parts.at[pl.ds(0, 63)], msem)


def on_device(sensitivity, residual_force, moments, zone_label, misfit):
    any_spec = pl.BlockSpec(memory_space=pl.ANY)
    vmem = pl.BlockSpec(memory_space=pltpu.VMEM)
    dma = pltpu.SemaphoreType.DMA
    h, g, z = pl.pallas_call(
        kernel,
        name="gauss_newton",
        out_shape=(
            jax.ShapeDtypeStruct((32, COLS), F32), jax.ShapeDtypeStruct((4, TILE), F32),
            jax.ShapeDtypeStruct((4, TILE), F32)),
        in_specs=[any_spec] * 5,
        out_specs=(vmem, vmem, vmem),
        scratch_shapes=[
            pltpu.VMEM((LAYERS + 1, 2 * TILE, 4 * TILE), BF),
            pltpu.VMEM((2 * LAYERS * TILE, TILE), BF),
            pltpu.VMEM((3, LAYERS * PLANE), BF),
            pltpu.VMEM((6, LAYERS, PLANE), F32),
            pltpu.VMEM((LAYERS, PLANE), jnp.int32),
            pltpu.VMEM((LAYERS, PLANE), F32),
            pltpu.VMEM((8, CHUNK, TILE), BF),
            pltpu.VMEM((8, CHUNK, TILE), BF),
            pltpu.VMEM((8, EDGE + PART, TILE), BF),
            pltpu.VMEM((8, PART, TILE), BF),
            pltpu.VMEM((3, WIDTH, KW), BF),
            pltpu.VMEM((LAYERS + 1, 3, COLS, 4 * TILE), F32),
            pltpu.VMEM((6, LAYERS, 16, TILE), F32),
            pltpu.VMEM((2, WIDTH, 256), F32),
            pltpu.VMEM((WIDTH, 256), F32),
            pltpu.VMEM((64, 16, TILE), F32),
            pltpu.VMEM((64, 16, TILE), F32),
            pltpu.VMEM((3, 8, TILE), F32),
            pltpu.VMEM((8, TILE), F32),
            pltpu.VMEM((8, 8, TILE), F32),
            pltpu.VMEM((8, 8, TILE), F32),
            dma((4,)), dma((8,)), dma((7,)), dma((8,)), dma((8,)), dma((8,)), dma((2,)),
            dma((3,)), dma((3,)), dma(()), dma(()),
        ],
        compiler_params=pltpu.CompilerParams(collective_id=0, has_side_effects=True, vmem_limit_bytes=67043328),
    )(sensitivity, residual_force, moments, zone_label, misfit)
    return h.T, g.reshape(WIDTH), z.reshape(WIDTH)


def solution(mesh):
    in_specs = (
        P(None, "col", "slab"),
        P(None, "slab"),
        P(None, "slab", None),
        P("slab", None),
        P("slab", None),
    )
    out_specs = (P("col", "slab"), P(), P())
    return jax.shard_map(
        on_device, mesh=mesh, in_specs=in_specs, out_specs=out_specs, check_vma=False
    )
```

time: 67.2 us -> 63.1 us (0.939)
  Pallas kernels: 62.6 us -> 58.4 us
  local copies, waits for them, and re-layouts: 2.21 us -> 3.8 us
  other arithmetic: 1.46 us -> 0 us
    pallas_call x1, Pallas kernels: 62.6 us -> 58.4 us  [on_device(): pl.pallas_call(kernel, name='gauss_newton', out_shape=(jax.ShapeDtypeStru...]
    unnamed x11 -> x3, local copies, waits for them, and re-layouts: 1.63 us -> 3.8 us
    another operation x1 -> x0, other arithmetic: 0.94 us -> none
where the time goes in v2:
time: 63.1 us; the launch traced here: 62.8 us
  Pallas kernels  58.4 us (93%)
  local copies, waits for them, and re-layouts  3.8 us (6%)
  between operations  0.64 us (1%)
    pallas_call x1, Pallas kernels, on_device(): pl.pallas_call(kernel, name='gauss_newton', out_shape=(jax.ShapeDtypeStru...  58.4 us
    unnamed x3, local copies, waits for them, and re-layouts  3.8 us

profile of v2, /device:TPU:6, one launch (start us, length us, event | category | flops | bytes accessed | tf_op | source)
XLA Modules:
  0.0 62.8 jit_solution(7022848508865389013)
XLA Ops:
  0.6 58.4 %gauss_newton.1 = (f32[32,64]{1,0:T(8,128)}, f32[4,128]{1,0:T(4,128)}, f32[4,128]{1,0:T(4,128)}) custom-call(bf16[3,64,4096]{2,1,0:T(8,128)(2,1)} %s_any.1, bf16[3,4096]{1,0:T(4,128)(2,1)} %res_any.1, f32[6,4,1024]{2,1,0:T(4,128)} %mom_any.1, s32[4,1024]{1,0:T(4,128)} %lab_any.1, f32[4,1024]{1,0:T(4,128)} %mis_any.1), custom_call_target="tpu_custom_call" | custom-call | tf_op jit(solution)/shard_map/gauss_newton/pallas_call | solution.py:387
  59.0 1.3 %copy.11 = f32[64,32]{0,1:T(8,128)} copy(f32[64,32]{0,1:T(8,128)} %bitcast.3) | data formatting | bytes 16384
  60.3 1.2 %copy.12 = f32[512]{0:T(512)} copy(f32[512]{0:T(512)} %bitcast.5) | data formatting | bytes 4096
  61.6 1.2 %copy.13 = f32[512]{0:T(512)} copy(f32[512]{0:T(512)} %bitcast.4) | data formatting | bytes 4096

commit v3 on v2

--- a/solution.py
+++ b/solution.py
@@ -31,7 +31,16 @@
     return jnp.where(shift == side, 2.0, jnp.where(shift == 1 - side, 1.0, 0.0))
 
 
-def fill_weights(w_ref, pick_ref):
+def fill_pick(pick_ref):
+    src, dst = iota((TILE, TILE), 0), iota((TILE, TILE), 1)
+    for h in range(2):
+        for l in range(LAYERS):
+            hit = (src == dst - 64 * h - GY * l) & (src < GY)
+            at = (h * LAYERS + l) * TILE
+            pick_ref[at:at + TILE, :] = jnp.where(hit, 1.0, 0.0).astype(BF)
+
+
+def fill_weights(w_ref):
     src, elem = iota((TILE, TILE), 0), iota((TILE, TILE), 1)
     ex, ey = elem // GY, lax.rem(elem, GY)
     sx, sy = src // GY, lax.rem(src, GY)
@@ -44,20 +53,15 @@
             for l in range(LAYERS + 1):
                 w_ref[l, 0:TILE, at:at + TILE] = near
                 w_ref[l, TILE:2 * TILE, at:at + TILE] = jnp.where(sx == l, far, 0.0).astype(BF)
-    for h in range(2):
-        for l in range(LAYERS):
-            hit = (src == elem - 64 * h - GY * l) & (src < GY)
-            at = (h * LAYERS + l) * TILE
-            pick_ref[at:at + TILE, :] = jnp.where(hit, 1.0, 0.0).astype(BF)
 
 
 def kernel(
     s_any, res_any, mom_any, lab_any, mis_any,
-    h_out, g_out, z_out,
+    out_ref,
     w_ref, pick_ref, res_ref, mom_ref, lab_ref, mis_ref,
-    stage, chunk, above, edges, img, fbuf, gbuf, hacc, hrecv, pack, parts,
+    sloc, hal, chunk, above, edges, img, fbuf, gbuf, hacc, hrecv, pack, parts,
     esrc, e0, e1, e2,
-    in_sem, st_sem, ss, rs, fs, fz, p0_sem, es, er, msem, rsem,
+    in_sem, own_sem, sa, sb, ra, rb, fs, fz, p0_sem, es, er, msem, rsem,
 ):
     s = lax.axis_index("slab")
     c = lax.axis_index("col")
@@ -85,15 +89,21 @@
     for to in (partner, lax.rem(s + 1, 16), below):
         pl.semaphore_signal(bar, inc=1, device_id=(to, c), device_id_type=MESH)
 
+    def wait_all(ref, sem):
+        pltpu.make_async_copy(ref, ref, sem).wait()
+
     def lanes(l, who):
         return pl.ds(pl.multiple_of(l * PLANE + who * TILE, TILE), TILE)
 
-    for who in range(8):
-        for l in range(LAYERS):
-            for k in range(3):
-                at = EDGE + l * PART + k * COLS
-                pltpu.make_async_copy(
-                    s_any.at[k, :, lanes(l, who)], stage.at[who, pl.ds(at, COLS), :], st_sem.at[who]).start()
+    def tile_rows(l, k):
+        return pl.ds(EDGE + l * PART + k * COLS, COLS)
+
+    whole = pltpu.make_async_copy(s_any, sloc, own_sem.at[0])
+    whole.start()
+    for l in range(LAYERS):
+        for k in range(3):
+            pltpu.make_async_copy(
+                s_any.at[k, :, lanes(l, c)], chunk.at[c, tile_rows(l, k), :], own_sem.at[1]).start()
     loads = [
         pltpu.make_async_copy(a, b, in_sem.at[i])
         for i, (a, b) in enumerate(((res_any, res_ref), (mom_any, mom_ref), (lab_any, lab_ref), (mis_any, mis_ref)))]
@@ -104,35 +114,59 @@
     def _():
         above[...] = jnp.zeros_like(above)
 
-    fill_weights(w_ref, pick_ref)
-    for who in range(8):
-        at = stage.at[who, pl.ds(EDGE, LAYERS * PART), :]
-        pltpu.make_async_copy(at, at, st_sem.at[who]).wait()
-
+    pl.semaphore_wait(bar, 66)
+
+    def send(i, l, sem, to):
+        who = col_peer(*OFFS[i])
+        for k in range(3):
+            pltpu.make_async_remote_copy(
+                src_ref=s_any.at[k, :, lanes(l, who)], dst_ref=chunk.at[c, tile_rows(l, k), :],
+                send_sem=sem, recv_sem=to.at[c], device_id=(s, who), device_id_type=MESH).start()
+
+    for i in range(7):
+        send(i, 0, sa, ra)
+    fill_pick(pick_ref)
+    whole.wait()
     for who in range(8):
         if who == 7:
-            stage[7, 0:EDGE, :] = jnp.zeros((EDGE, TILE), BF)
+            hal[7] = jnp.zeros((EDGE, TILE), BF)
         else:
-            tiles = [
-                jnp.concatenate([
-                    stage[who + 1, EDGE + l * PART + k * COLS + 32 * h:EDGE + l * PART + k * COLS + 32 * h + 32, :]
-                    for k in range(3)], axis=0)
-                for h in range(2) for l in range(LAYERS)]
+            tiles = []
+            for h in range(2):
+                for l in range(LAYERS):
+                    at = l * PLANE + (who + 1) * TILE
+                    tiles.append(jnp.concatenate(
+                        [sloc[k, 32 * h:32 * h + 32, at:at + TILE] for k in range(3)], axis=0))
             got = jnp.dot(jnp.concatenate(tiles, axis=1), pick_ref[...], preferred_element_type=F32)
-            stage[who, 0:EDGE, :] = got.astype(BF)
-    pltpu.make_async_copy(stage.at[c], chunk.at[c], rs.at[c]).start()
-
-    pl.semaphore_wait(bar, 66)
-
-    def send(i):
+            hal[who] = got.astype(BF)
+    for i in range(7):
         who = col_peer(*OFFS[i])
+        pltpu.make_async_remote_copy(
+            src_ref=hal.at[who], dst_ref=chunk.at[c, pl.ds(0, EDGE), :],
+            send_sem=sa, recv_sem=ra.at[c], device_id=(s, who), device_id_type=MESH).start()
+    for i in range(7):
+        for l in range(1, LAYERS):
+            send(i, l, sb, rb)
+    chunk[c, 0:EDGE, :] = hal[c]
+    wait_all(chunk.at[c, pl.ds(EDGE, LAYERS * PART), :], own_sem.at[1])
+
+    def forward(j):
+        src = order[j]
         return pltpu.make_async_remote_copy(
-            src_ref=stage.at[who], dst_ref=chunk.at[c], send_sem=ss.at[i], recv_sem=rs.at[c],
-            device_id=(s, who), device_id_type=MESH)
-
-    for i in range(7):
-        send(i).start()
-
+            src_ref=chunk.at[src, pl.ds(0, EDGE + PART), :], dst_ref=above.at[src],
+            send_sem=fs.at[j], recv_sem=fz.at[src], device_id=(below, c), device_id_type=MESH)
+
+    def arrive(j):
+        src = order[j]
+        if j > 0:
+            wait_all(chunk.at[src, pl.ds(0, EDGE + PART), :], ra.at[src])
+
+        @pl.when(s > 0)
+        def _():
+            forward(j).start()
+
+    arrive(0)
+    fill_weights(w_ref)
     for load in loads:
         load.wait()
     ctile = pl.ds(pl.multiple_of(c * TILE, TILE), TILE)
@@ -142,8 +176,7 @@
     grad = None
     for k in range(3):
         for l in range(LAYERS):
-            at = EDGE + l * PART + k * COLS
-            rhs = jnp.concatenate([stage[who, at:at + COLS, :] for who in range(8)], axis=1)
+            rhs = sloc[k, :, l * PLANE:(l + 1) * PLANE]
             row = res_ref[k:k + 1, l * PLANE:(l + 1) * PLANE].astype(F32)
             lhs = jnp.broadcast_to(row, (16, PLANE)).astype(BF)
             got = lax.dot_general(lhs, rhs, NT, preferred_element_type=F32)
@@ -186,9 +219,6 @@
             src_ref=esrc.at[2], dst_ref=e2.at[c], send_sem=es.at[2], recv_sem=er.at[2],
             device_id=(s, col_peer(*OFFS[i])), device_id_type=MESH)
 
-    def wait_all(ref, sem):
-        pltpu.make_async_copy(ref, ref, sem).wait()
-
     small0.start()
 
     lane = iota((16, TILE), 1)
@@ -196,22 +226,10 @@
     inside = lane >= GY
     edge_lane = iota((32, TILE), 1)
 
-    def arrive(j):
-        src = order[j]
-        wait_all(chunk.at[src], rs.at[src])
-
-        @pl.when(s > 0)
-        def _():
-            forward(j).start()
-
-    def forward(j):
-        src = order[j]
-        return pltpu.make_async_remote_copy(
-            src_ref=chunk.at[src, pl.ds(0, EDGE + PART), :], dst_ref=above.at[src],
-            send_sem=fs.at[j], recv_sem=fz.at[src], device_id=(below, c), device_id_type=MESH)
-
     def block(j):
         src = order[j]
+        if j > 0:
+            wait_all(chunk.at[src, pl.ds(EDGE + PART, 3 * PART), :], rb.at[src])
 
         @pl.when(s < 15)
         def _():
@@ -277,26 +295,18 @@
             for k in range(3):
                 img[k, dest, KW - TILE:KW] = edge[k].astype(BF)
 
-    arrive(0)
-    for j in range(8):
-        if j < 7:
-            arrive(j + 1)
+    for j in range(1, 4):
+        arrive(j)
+    block(0)
+    small0.wait_recv()
+    esrc[1] = esrc[0] + e0[...]
+    for i in range(7):
+        small1(i).start()
+    e1[d] = esrc[1]
+    for j in range(4, 8):
+        arrive(j)
+    for j in range(1, 8):
         block(j)
-        if j == 1:
-            small0.wait_recv()
-            esrc[1] = esrc[0] + e0[...]
-            for i in range(7):
-                small1(i).start()
-            e1[d] = esrc[1]
-        if j == 4:
-            wait_all(e1.at[pl.ds(0, 7)], er.at[1])
-            total = e1[0]
-            for who in range(1, 8):
-                total = total + e1[who]
-            esrc[2] = total
-            for i in range(7):
-                small2(i).start()
-            e2[c] = total
 
     def panel(half):
         total = None
@@ -320,6 +330,14 @@
         src_ref=hacc.at[other], dst_ref=hrecv, send_sem=p0_sem.at[0], recv_sem=p0_sem.at[1],
         device_id=(partner, c), device_id_type=MESH)
     swap.start()
+    wait_all(e1.at[pl.ds(0, 7)], er.at[1])
+    total = e1[0]
+    for who in range(1, 8):
+        total = total + e1[who]
+    esrc[2] = total
+    for i in range(7):
+        small2(i).start()
+    e2[c] = total
     panel(core)
     swap.wait_recv()
 
@@ -354,25 +372,25 @@
     zone = e2[0]
     for who in range(1, 8):
         zone = zone + e2[who]
-    z_out[...] = zone[4:8] * (WIDTH / 65536)
+    out_ref[36:40, :] = zone[4:8] * (WIDTH / 65536)
     left = iota((1, TILE), 1) < COLS
     for t in range(4):
-        g_out[t:t + 1, :] = jnp.where(left, e2[2 * t, 0:1, :], pltpu.roll(e2[2 * t + 1, 0:1, :], COLS, 1))
+        out_ref[32 + t:33 + t, :] = jnp.where(left, e2[2 * t, 0:1, :], pltpu.roll(e2[2 * t + 1, 0:1, :], COLS, 1))
 
     wait_all(parts.at[pl.ds(0, 63)], rsem)
     total = parts[0]
     for who in range(1, 64):
         total = total + parts[who]
     rows = [pltpu.roll(total, TILE - 32 * g, 1) if g else total for g in range(4)]
-    h_out[...] = jnp.transpose(jnp.concatenate(rows, axis=0))[0:32, :]
+    out_ref[0:32, 0:COLS] = jnp.transpose(jnp.concatenate(rows, axis=0))[0:32, :]
 
     @pl.when(s > 0)
     def _():
         for j in range(8):
             forward(j).wait_send()
 
-    for i in range(7):
-        send(i).wait_send()
+    wait_all(chunk.at[pl.ds(0, 7), pl.ds(0, EDGE + PART), :], sa)
+    wait_all(chunk.at[pl.ds(0, 7), pl.ds(EDGE + PART, 3 * PART), :], sb)
     small0.wait_send()
     wait_all(e1.at[pl.ds(0, 7)], es.at[1])
     wait_all(e2.at[pl.ds(0, 7)], es.at[2])
@@ -384,14 +402,12 @@
     any_spec = pl.BlockSpec(memory_space=pl.ANY)
     vmem = pl.BlockSpec(memory_space=pltpu.VMEM)
     dma = pltpu.SemaphoreType.DMA
-    h, g, z = pl.pallas_call(
+    out = pl.pallas_call(
         kernel,
         name="gauss_newton",
-        out_shape=(
-            jax.ShapeDtypeStruct((32, COLS), F32), jax.ShapeDtypeStruct((4, TILE), F32),
-            jax.ShapeDtypeStruct((4, TILE), F32)),
+        out_shape=jax.ShapeDtypeStruct((40, TILE), F32),
         in_specs=[any_spec] * 5,
-        out_specs=(vmem, vmem, vmem),
+        out_specs=vmem,
         scratch_shapes=[
             pltpu.VMEM((LAYERS + 1, 2 * TILE, 4 * TILE), BF),
             pltpu.VMEM((2 * LAYERS * TILE, TILE), BF),
@@ -399,7 +415,8 @@
             pltpu.VMEM((6, LAYERS, PLANE), F32),
             pltpu.VMEM((LAYERS, PLANE), jnp.int32),
             pltpu.VMEM((LAYERS, PLANE), F32),
-            pltpu.VMEM((8, CHUNK, TILE), BF),
+            pltpu.VMEM((3, COLS, LAYERS * PLANE), BF),
+            pltpu.VMEM((8, EDGE, TILE), BF),
             pltpu.VMEM((8, CHUNK, TILE), BF),
             pltpu.VMEM((8, EDGE + PART, TILE), BF),
             pltpu.VMEM((8, PART, TILE), BF),
@@ -414,12 +431,12 @@
             pltpu.VMEM((8, TILE), F32),
             pltpu.VMEM((8, 8, TILE), F32),
             pltpu.VMEM((8, 8, TILE), F32),
-            dma((4,)), dma((8,)), dma((7,)), dma((8,)), dma((8,)), dma((8,)), dma((2,)),
+            dma((4,)), dma((2,)), dma(()), dma(()), dma((8,)), dma((8,)), dma((8,)), dma((8,)), dma((2,)),
             dma((3,)), dma((3,)), dma(()), dma(()),
         ],
         compiler_params=pltpu.CompilerParams(collective_id=0, has_side_effects=True, vmem_limit_bytes=67043328),
     )(sensitivity, residual_force, moments, zone_label, misfit)
-    return h.T, g.reshape(WIDTH), z.reshape(WIDTH)
+    return out[0:32, 0:COLS].T, out[32:36].reshape(WIDTH), out[36:40].reshape(WIDTH)
 
 
 def solution(mesh):

time: 63.1 us -> 60.6 us (0.960)
  Pallas kernels: 58.4 us -> 57 us
  local copies, waits for them, and re-layouts: 3.8 us -> 2.66 us
    unnamed x3 -> x0, local copies, waits for them, and re-layouts: 3.8 us -> none
    pallas_call x1, Pallas kernels: 58.4 us -> 57 us  [on_device(): pl.pallas_call(kernel, name='gauss_newton', out_shape=jax.ShapeDtypeStruc...]
    reshape x0 -> x1, local copies, waits for them, and re-layouts: none -> 1.33 us  [on_device(): out[36:40].reshape(WIDTH)]
    transpose x0 -> x1, local copies, waits for them, and re-layouts: none -> 1.32 us  [on_device(): out[0:32, 0:COLS]]
where the time goes in v3:
time: 60.6 us; the launch traced here: 60.3 us
  Pallas kernels  57 us (94%)
  local copies, waits for them, and re-layouts  2.66 us (4%)
  between operations  0.64 us (1%)
    pallas_call x1, Pallas kernels, on_device(): pl.pallas_call(kernel, name='gauss_newton', out_shape=jax.ShapeDtypeStruc...  57 us
    reshape x1, local copies, waits for them, and re-layouts, on_device(): out[36:40].reshape(WIDTH)  1.33 us
    transpose x1, local copies, waits for them, and re-layouts, on_device(): out[0:32, 0:COLS]  1.32 us

profile of v3, /device:TPU:6, one launch (start us, length us, event | category | flops | bytes accessed | tf_op | source)
XLA Modules:
  0.0 60.3 jit_solution(8054357225352697254)
XLA Ops:
  0.6 57.0 %gauss_newton.1 = f32[40,128]{1,0:T(8,128)} custom-call(bf16[3,64,4096]{2,1,0:T(8,128)(2,1)} %s_any.1, bf16[3,4096]{1,0:T(4,128)(2,1)} %res_any.1, f32[6,4,1024]{2,1,0:T(4,128)} %mom_any.1, s32[4,1024]{1,0:T(4,128)} %lab_any.1, f32[4,1024]{1,0:T(4,128)} %mis_any.1), custom_call_target="tpu_custom_call" | custom-call | tf_op jit(solution)/shard_map/gauss_newton/pallas_call | solution.py:405
  57.7 1.3 %slice_bitcast_fusion.1 = (f32[512]{0:T(512)}, f32[512]{0:T(512)}) fusion(f32[40,128]{1,0:T(8,128)} %gauss_newton.1), kind=kLoop, calls=%fused_computation.1 | loop fusion | bytes 8192 | tf_op jit(solution)/shard_map/reshape | solution.py:439
  59.0 1.3 %slice_bitcast_fusion = f32[64,32]{0,1:T(8,128)} fusion(f32[40,128]{1,0:T(8,128)} %gauss_newton.1), kind=kLoop, calls=%fused_computation | loop fusion | bytes 16384 | tf_op jit(solution)/shard_map/transpose | solution.py:439

commit v4 on v3

--- a/solution.py
+++ b/solution.py
@@ -61,7 +61,7 @@
     w_ref, pick_ref, res_ref, mom_ref, lab_ref, mis_ref,
     sloc, hal, chunk, above, edges, img, fbuf, gbuf, hacc, hrecv, pack, parts,
     esrc, e0, e1, e2,
-    in_sem, own_sem, sa, sb, ra, rb, fs, fz, p0_sem, es, er, msem, rsem,
+    in_sem, own_sem, sa, sb, ra, rb, fs, fz, p0_sem, p1_sem, es, er, msem, rsem,
 ):
     s = lax.axis_index("slab")
     c = lax.axis_index("col")
@@ -144,9 +144,6 @@
         pltpu.make_async_remote_copy(
             src_ref=hal.at[who], dst_ref=chunk.at[c, pl.ds(0, EDGE), :],
             send_sem=sa, recv_sem=ra.at[c], device_id=(s, who), device_id_type=MESH).start()
-    for i in range(7):
-        for l in range(1, LAYERS):
-            send(i, l, sb, rb)
     chunk[c, 0:EDGE, :] = hal[c]
     wait_all(chunk.at[c, pl.ds(EDGE, LAYERS * PART), :], own_sem.at[1])
 
@@ -295,9 +292,17 @@
             for k in range(3):
                 img[k, dest, KW - TILE:KW] = edge[k].astype(BF)
 
+    wait_all(chunk.at[pl.ds(0, 7), pl.ds(0, EDGE + PART), :], sa)
+    for i in range(3):
+        for l in range(1, LAYERS):
+            send(i, l, sb, rb)
     for j in range(1, 4):
         arrive(j)
     block(0)
+    wait_all(chunk.at[pl.ds(0, 3), pl.ds(EDGE + PART, 3 * PART), :], sb)
+    for i in range(3, 7):
+        for l in range(1, LAYERS):
+            send(i, l, sb, rb)
     small0.wait_recv()
     esrc[1] = esrc[0] + e0[...]
     for i in range(7):
@@ -326,10 +331,14 @@
 
     other = 1 - core
     panel(other)
-    swap = pltpu.make_async_remote_copy(
-        src_ref=hacc.at[other], dst_ref=hrecv, send_sem=p0_sem.at[0], recv_sem=p0_sem.at[1],
-        device_id=(partner, c), device_id_type=MESH)
-    swap.start()
+    def swap(i):
+        rows = pl.ds(pl.multiple_of(lax.rem(c + i, 8) * COLS, COLS), COLS)
+        return pltpu.make_async_remote_copy(
+            src_ref=hacc.at[other, rows, :], dst_ref=hrecv.at[rows, :], send_sem=p0_sem.at[i], recv_sem=p1_sem.at[i],
+            device_id=(partner, c), device_id_type=MESH)
+
+    for i in range(8):
+        swap(i).start()
     wait_all(e1.at[pl.ds(0, 7)], er.at[1])
     total = e1[0]
     for who in range(1, 8):
@@ -339,12 +348,12 @@
         small2(i).start()
     e2[c] = total
     panel(core)
-    swap.wait_recv()
 
     me = c * 8 + d
     group = lane // 32
     for i in range(8):
         to_c = lax.rem(c + i, 8)
+        swap(i).wait_recv()
         sums = []
         for g in range(4):
             rows = pl.ds(pl.multiple_of(to_c * COLS + 16 * g, 16), 16)
@@ -389,12 +398,12 @@
         for j in range(8):
             forward(j).wait_send()
 
-    wait_all(chunk.at[pl.ds(0, 7), pl.ds(0, EDGE + PART), :], sa)
-    wait_all(chunk.at[pl.ds(0, 7), pl.ds(EDGE + PART, 3 * PART), :], sb)
+    wait_all(chunk.at[pl.ds(0, 4), pl.ds(EDGE + PART, 3 * PART), :], sb)
     small0.wait_send()
     wait_all(e1.at[pl.ds(0, 7)], es.at[1])
     wait_all(e2.at[pl.ds(0, 7)], es.at[2])
-    swap.wait_send()
+    for i in range(8):
+        swap(i).wait_send()
     wait_all(parts.at[pl.ds(0, 63)], msem)
 
 
@@ -431,7 +440,7 @@
             pltpu.VMEM((8, TILE), F32),
             pltpu.VMEM((8, 8, TILE), F32),
             pltpu.VMEM((8, 8, TILE), F32),
-            dma((4,)), dma((2,)), dma(()), dma(()), dma((8,)), dma((8,)), dma((8,)), dma((8,)), dma((2,)),
+            dma((4,)), dma((2,)), dma(()), dma(()), dma((8,)), dma((8,)), dma((8,)), dma((8,)), dma((8,)), dma((8,)),
             dma((3,)), dma((3,)), dma(()), dma(()),
         ],
         compiler_params=pltpu.CompilerParams(collective_id=0, has_side_effects=True, vmem_limit_bytes=67043328),

time: 60.6 us -> 57.6 us (0.950)
  Pallas kernels: 57 us -> 53.9 us
    pallas_call x1, Pallas kernels: 57 us -> 53.9 us  [on_device(): pl.pallas_call(kernel, name='gauss_newton', out_shape=jax.ShapeDtypeStruc...]
where the time goes in v4:
time: 57.6 us; the launch traced here: 57.2 us
  Pallas kernels  53.9 us (94%)
  local copies, waits for them, and re-layouts  2.66 us (5%)
  between operations  0.64 us (1%)
    pallas_call x1, Pallas kernels, on_device(): pl.pallas_call(kernel, name='gauss_newton', out_shape=jax.ShapeDtypeStruc...  53.9 us
    reshape x1, local copies, waits for them, and re-layouts, on_device(): out[36:40].reshape(WIDTH)  1.33 us
    transpose x1, local copies, waits for them, and re-layouts, on_device(): out[0:32, 0:COLS]  1.32 us

profile of v4, /device:TPU:6, one launch (start us, length us, event | category | flops | bytes accessed | tf_op | source)
XLA Modules:
  0.0 57.2 jit_solution(12844003412673381314)
XLA Ops:
  0.6 53.9 %gauss_newton.1 = f32[40,128]{1,0:T(8,128)} custom-call(bf16[3,64,4096]{2,1,0:T(8,128)(2,1)} %s_any.1, bf16[3,4096]{1,0:T(4,128)(2,1)} %res_any.1, f32[6,4,1024]{2,1,0:T(4,128)} %mom_any.1, s32[4,1024]{1,0:T(4,128)} %lab_any.1, f32[4,1024]{1,0:T(4,128)} %mis_any.1), custom_call_target="tpu_custom_call" | custom-call | tf_op jit(solution)/shard_map/gauss_newton/pallas_call | solution.py:414
  54.5 1.3 %slice_bitcast_fusion.1 = (f32[512]{0:T(512)}, f32[512]{0:T(512)}) fusion(f32[40,128]{1,0:T(8,128)} %gauss_newton.1), kind=kLoop, calls=%fused_computation.1 | loop fusion | bytes 8192 | tf_op jit(solution)/shard_map/reshape | solution.py:448
  55.8 1.3 %slice_bitcast_fusion = f32[64,32]{0,1:T(8,128)} fusion(f32[40,128]{1,0:T(8,128)} %gauss_newton.1), kind=kLoop, calls=%fused_computation | loop fusion | bytes 16384 | tf_op jit(solution)/shard_map/transpose | solution.py:448

commit v5 on v4

--- a/solution.py
+++ b/solution.py
@@ -82,10 +82,9 @@
     partner = s + 1 - 2 * core
     below = lax.rem(s + 15, 16)
     bar = pltpu.get_barrier_semaphore()
-    for k in range(1, 64):
-        to_c = lax.rem(c + k // 8, 8)
-        to_d = lax.rem(d + k, 8)
-        pl.semaphore_signal(bar, inc=1, device_id=(to_d * 2 + core, to_c), device_id_type=MESH)
+    for dx, dy in OFFS:
+        pl.semaphore_signal(bar, inc=1, device_id=(s, col_peer(dx, dy)), device_id_type=MESH)
+        pl.semaphore_signal(bar, inc=1, device_id=(slab_peer(dx, dy), c), device_id_type=MESH)
     for to in (partner, lax.rem(s + 1, 16), below):
         pl.semaphore_signal(bar, inc=1, device_id=(to, c), device_id_type=MESH)
 
@@ -114,7 +113,7 @@
     def _():
         above[...] = jnp.zeros_like(above)
 
-    pl.semaphore_wait(bar, 66)
+    pl.semaphore_wait(bar, 17)
 
     def send(i, l, sem, to):
         who = col_peer(*OFFS[i])
@@ -293,16 +292,24 @@
                 img[k, dest, KW - TILE:KW] = edge[k].astype(BF)
 
     wait_all(chunk.at[pl.ds(0, 7), pl.ds(0, EDGE + PART), :], sa)
-    for i in range(3):
-        for l in range(1, LAYERS):
-            send(i, l, sb, rb)
+    groups = ((0, 1, 2), (3,), (4,), (5,), (6,))
+
+    def send_group(g):
+        for i in groups[g]:
+            for l in range(1, LAYERS):
+                send(i, l, sb.at[g], rb)
+
+    def group_left(g):
+        wait_all(chunk.at[pl.ds(0, len(groups[g])), pl.ds(EDGE + PART, 3 * PART), :], sb.at[g])
+
+    send_group(0)
+    send_group(1)
+    send_group(2)
     for j in range(1, 4):
         arrive(j)
     block(0)
-    wait_all(chunk.at[pl.ds(0, 3), pl.ds(EDGE + PART, 3 * PART), :], sb)
-    for i in range(3, 7):
-        for l in range(1, LAYERS):
-            send(i, l, sb, rb)
+    group_left(0)
+    send_group(3)
     small0.wait_recv()
     esrc[1] = esrc[0] + e0[...]
     for i in range(7):
@@ -311,7 +318,19 @@
     for j in range(4, 8):
         arrive(j)
     for j in range(1, 8):
+        if j == 3:
+            group_left(1)
+            send_group(4)
         block(j)
+        if j == 4:
+            wait_all(e1.at[pl.ds(0, 7)], er.at[1])
+            total = e1[0]
+            for who in range(1, 8):
+                total = total + e1[who]
+            esrc[2] = total
+            for i in range(7):
+                small2(i).start()
+            e2[c] = total
 
     def panel(half):
         total = None
@@ -339,15 +358,9 @@
 
     for i in range(8):
         swap(i).start()
-    wait_all(e1.at[pl.ds(0, 7)], er.at[1])
-    total = e1[0]
-    for who in range(1, 8):
-        total = total + e1[who]
-    esrc[2] = total
-    for i in range(7):
-        small2(i).start()
-    e2[c] = total
     panel(core)
+
+    wait_all(e2.at[pl.ds(0, 7)], er.at[2])
 
     me = c * 8 + d
     group = lane // 32
@@ -377,7 +390,6 @@
                 device_id=(to_d * 2 + core, to_c), device_id_type=MESH).start()
     parts[me] = pack[me]
 
-    wait_all(e2.at[pl.ds(0, 7)], er.at[2])
     zone = e2[0]
     for who in range(1, 8):
         zone = zone + e2[who]
@@ -398,7 +410,9 @@
         for j in range(8):
             forward(j).wait_send()
 
-    wait_all(chunk.at[pl.ds(0, 4), pl.ds(EDGE + PART, 3 * PART), :], sb)
+    group_left(2)
+    group_left(3)
+    group_left(4)
     small0.wait_send()
     wait_all(e1.at[pl.ds(0, 7)], es.at[1])
     wait_all(e2.at[pl.ds(0, 7)], es.at[2])
@@ -440,7 +454,7 @@
             pltpu.VMEM((8, TILE), F32),
             pltpu.VMEM((8, 8, TILE), F32),
             pltpu.VMEM((8, 8, TILE), F32),
-            dma((4,)), dma((2,)), dma(()), dma(()), dma((8,)), dma((8,)), dma((8,)), dma((8,)), dma((8,)), dma((8,)),
+            dma((4,)), dma((2,)), dma(()), dma((5,)), dma((8,)), dma((8,)), dma((8,)), dma((8,)), dma((8,)), dma((8,)),
             dma((3,)), dma((3,)), dma(()), dma(()),
         ],
         compiler_params=pltpu.CompilerParams(collective_id=0, has_side_effects=True, vmem_limit_bytes=67043328),

time: 57.6 us -> 55.1 us (0.957)
  Pallas kernels: 53.9 us -> 51.5 us
    pallas_call x1, Pallas kernels: 53.9 us -> 51.5 us  [on_device(): pl.pallas_call(kernel, name='gauss_newton', out_shape=jax.ShapeDtypeStruc...]
where the time goes in v5:
time: 55.1 us; the launch traced here: 54.7 us
  Pallas kernels  51.5 us (93%)
  local copies, waits for them, and re-layouts  2.66 us (5%)
  between operations  0.64 us (1%)
    pallas_call x1, Pallas kernels, on_device(): pl.pallas_call(kernel, name='gauss_newton', out_shape=jax.ShapeDtypeStruc...  51.5 us
    reshape x1, local copies, waits for them, and re-layouts, on_device(): out[36:40].reshape(WIDTH)  1.33 us
    transpose x1, local copies, waits for them, and re-layouts, on_device(): out[0:32, 0:COLS]  1.32 us

profile of v5, /device:TPU:6, one launch (start us, length us, event | category | flops | bytes accessed | tf_op | source)
XLA Modules:
  0.0 54.7 jit_solution(4387809290827673906)
XLA Ops:
  0.6 51.5 %gauss_newton.1 = f32[40,128]{1,0:T(8,128)} custom-call(bf16[3,64,4096]{2,1,0:T(8,128)(2,1)} %s_any.1, bf16[3,4096]{1,0:T(4,128)(2,1)} %res_any.1, f32[6,4,1024]{2,1,0:T(4,128)} %mom_any.1, s32[4,1024]{1,0:T(4,128)} %lab_any.1, f32[4,1024]{1,0:T(4,128)} %mis_any.1), custom_call_target="tpu_custom_call" | custom-call | tf_op jit(solution)/shard_map/gauss_newton/pallas_call | solution.py:428
  52.1 1.3 %slice_bitcast_fusion.1 = (f32[512]{0:T(512)}, f32[512]{0:T(512)}) fusion(f32[40,128]{1,0:T(8,128)} %gauss_newton.1), kind=kLoop, calls=%fused_computation.1 | loop fusion | bytes 8192 | tf_op jit(solution)/shard_map/reshape | solution.py:462
  53.4 1.3 %slice_bitcast_fusion = f32[64,32]{0,1:T(8,128)} fusion(f32[40,128]{1,0:T(8,128)} %gauss_newton.1), kind=kLoop, calls=%fused_computation | loop fusion | bytes 16384 | tf_op jit(solution)/shard_map/transpose | solution.py:462

commit v6 on v5

--- a/solution.py
+++ b/solution.py
@@ -20,6 +20,7 @@
 BF = jnp.bfloat16
 F32 = jnp.float32
 NT = (((1,), (1,)), ((), ()))
+FAR = ((1, 2), (1, 1), (1, 3), (0, 2), (1, 0), (0, 1), (0, 3), (0, 0))
 OFFS = ((0, 1), (0, 3), (1, 0), (0, 2), (1, 1), (1, 3), (1, 2))
 
 
@@ -351,7 +352,7 @@
     other = 1 - core
     panel(other)
     def swap(i):
-        rows = pl.ds(pl.multiple_of(lax.rem(c + i, 8) * COLS, COLS), COLS)
+        rows = pl.ds(pl.multiple_of(col_peer(*FAR[i]) * COLS, COLS), COLS)
         return pltpu.make_async_remote_copy(
             src_ref=hacc.at[other, rows, :], dst_ref=hrecv.at[rows, :], send_sem=p0_sem.at[i], recv_sem=p1_sem.at[i],
             device_id=(partner, c), device_id_type=MESH)
@@ -365,7 +366,7 @@
     me = c * 8 + d
     group = lane // 32
     for i in range(8):
-        to_c = lax.rem(c + i, 8)
+        to_c = col_peer(*FAR[i])
         swap(i).wait_recv()
         sums = []
         for g in range(4):
@@ -382,9 +383,9 @@
                 packed = piece if packed is None else jnp.where(group == g, piece, packed)
             pack[to_c * 8 + e] = packed
         for j in range(8):
-            if i + j == 0:
+            if i + j == 14:
                 continue
-            to_d = lax.rem(d + j, 8)
+            to_d = slab_peer(*FAR[j]) // 2
             pltpu.make_async_remote_copy(
                 src_ref=pack.at[to_c * 8 + to_d], dst_ref=parts.at[me], send_sem=msem, recv_sem=rsem,
                 device_id=(to_d * 2 + core, to_c), device_id_type=MESH).start()

time: 55.1 us -> 54.4 us (0.987)
  Pallas kernels: 51.5 us -> 50.5 us
    pallas_call x1, Pallas kernels: 51.5 us -> 50.5 us  [on_device(): pl.pallas_call(kernel, name='gauss_newton', out_shape=jax.ShapeDtypeStruc...]
where the time goes in v6:
time: 54.4 us; the launch traced here: 53.8 us
  Pallas kernels  50.5 us (93%)
  local copies, waits for them, and re-layouts  2.66 us (5%)
  between operations  0.64 us (1%)
    pallas_call x1, Pallas kernels, on_device(): pl.pallas_call(kernel, name='gauss_newton', out_shape=jax.ShapeDtypeStruc...  50.5 us
    reshape x1, local copies, waits for them, and re-layouts, on_device(): out[36:40].reshape(WIDTH)  1.33 us
    transpose x1, local copies, waits for them, and re-layouts, on_device(): out[0:32, 0:COLS]  1.32 us

profile of v6, /device:TPU:6, one launch (start us, length us, event | category | flops | bytes accessed | tf_op | source)
XLA Modules:
  0.0 53.8 jit_solution(1052474851005413739)
XLA Ops:
  0.6 50.5 %gauss_newton.1 = f32[40,128]{1,0:T(8,128)} custom-call(bf16[3,64,4096]{2,1,0:T(8,128)(2,1)} %s_any.1, bf16[3,4096]{1,0:T(4,128)(2,1)} %res_any.1, f32[6,4,1024]{2,1,0:T(4,128)} %mom_any.1, s32[4,1024]{1,0:T(4,128)} %lab_any.1, f32[4,1024]{1,0:T(4,128)} %mis_any.1), custom_call_target="tpu_custom_call" | custom-call | tf_op jit(solution)/shard_map/gauss_newton/pallas_call | solution.py:429
  51.1 1.3 %slice_bitcast_fusion.1 = (f32[512]{0:T(512)}, f32[512]{0:T(512)}) fusion(f32[40,128]{1,0:T(8,128)} %gauss_newton.1), kind=kLoop, calls=%fused_computation.1 | loop fusion | bytes 8192 | tf_op jit(solution)/shard_map/reshape | solution.py:463
  52.4 1.3 %slice_bitcast_fusion = f32[64,32]{0,1:T(8,128)} fusion(f32[40,128]{1,0:T(8,128)} %gauss_newton.1), kind=kLoop, calls=%fused_computation | loop fusion | bytes 16384 | tf_op jit(solution)/shard_map/transpose | solution.py:463

commit v7 on v6

--- a/solution.py
+++ b/solution.py
@@ -144,6 +144,17 @@
         pltpu.make_async_remote_copy(
             src_ref=hal.at[who], dst_ref=chunk.at[c, pl.ds(0, EDGE), :],
             send_sem=sa, recv_sem=ra.at[c], device_id=(s, who), device_id_type=MESH).start()
+    groups = ((0, 1, 2), (3,), (4,), (5,), (6,))
+
+    def send_group(g):
+        for i in groups[g]:
+            for l in range(1, LAYERS):
+                send(i, l, sb.at[g], rb)
+
+    def group_left(g):
+        wait_all(chunk.at[pl.ds(0, len(groups[g])), pl.ds(EDGE + PART, 3 * PART), :], sb.at[g])
+
+    send_group(0)
     chunk[c, 0:EDGE, :] = hal[c]
     wait_all(chunk.at[c, pl.ds(EDGE, LAYERS * PART), :], own_sem.at[1])
 
@@ -293,17 +304,6 @@
                 img[k, dest, KW - TILE:KW] = edge[k].astype(BF)
 
     wait_all(chunk.at[pl.ds(0, 7), pl.ds(0, EDGE + PART), :], sa)
-    groups = ((0, 1, 2), (3,), (4,), (5,), (6,))
-
-    def send_group(g):
-        for i in groups[g]:
-            for l in range(1, LAYERS):
-                send(i, l, sb.at[g], rb)
-
-    def group_left(g):
-        wait_all(chunk.at[pl.ds(0, len(groups[g])), pl.ds(EDGE + PART, 3 * PART), :], sb.at[g])
-
-    send_group(0)
     send_group(1)
     send_group(2)
     for j in range(1, 4):

time: 54.4 us -> 54.4 us (level)
  no operation moved by 1% of the time
where the time goes in v7:
time: 54.4 us; the launch traced here: 53.6 us
  Pallas kernels  50.3 us (92%)
  local copies, waits for them, and re-layouts  2.66 us (5%)
  between operations  0.64 us (1%)
    pallas_call x1, Pallas kernels, on_device(): pl.pallas_call(kernel, name='gauss_newton', out_shape=jax.ShapeDtypeStruc...  50.3 us
    reshape x1, local copies, waits for them, and re-layouts, on_device(): out[36:40].reshape(WIDTH)  1.33 us
    transpose x1, local copies, waits for them, and re-layouts, on_device(): out[0:32, 0:COLS]  1.32 us

profile of v7, /device:TPU:6, one launch (start us, length us, event | category | flops | bytes accessed | tf_op | source)
XLA Modules:
  0.0 53.6 jit_solution(16666777689525955582)
XLA Ops:
  0.6 50.3 %gauss_newton.1 = f32[40,128]{1,0:T(8,128)} custom-call(bf16[3,64,4096]{2,1,0:T(8,128)(2,1)} %s_any.1, bf16[3,4096]{1,0:T(4,128)(2,1)} %res_any.1, f32[6,4,1024]{2,1,0:T(4,128)} %mom_any.1, s32[4,1024]{1,0:T(4,128)} %lab_any.1, f32[4,1024]{1,0:T(4,128)} %mis_any.1), custom_call_target="tpu_custom_call" | custom-call | tf_op jit(solution)/shard_map/gauss_newton/pallas_call | solution.py:429
  50.9 1.3 %slice_bitcast_fusion.1 = (f32[512]{0:T(512)}, f32[512]{0:T(512)}) fusion(f32[40,128]{1,0:T(8,128)} %gauss_newton.1), kind=kLoop, calls=%fused_computation.1 | loop fusion | bytes 8192 | tf_op jit(solution)/shard_map/reshape | solution.py:463
  52.3 1.3 %slice_bitcast_fusion = f32[64,32]{0,1:T(8,128)} fusion(f32[40,128]{1,0:T(8,128)} %gauss_newton.1), kind=kLoop, calls=%fused_computation | loop fusion | bytes 16384 | tf_op jit(solution)/shard_map/transpose | solution.py:463

commit v8 on v6

--- a/solution.py
+++ b/solution.py
@@ -114,6 +114,7 @@
     def _():
         above[...] = jnp.zeros_like(above)
 
+    fill_pick(pick_ref)
     pl.semaphore_wait(bar, 17)
 
     def send(i, l, sem, to):
@@ -125,7 +126,6 @@
 
     for i in range(7):
         send(i, 0, sa, ra)
-    fill_pick(pick_ref)
     whole.wait()
     for who in range(8):
         if who == 7:

time: 54.4 us -> 54.4 us (level)
  no operation moved by 1% of the time
where the time goes in v8:
time: 54.4 us; the launch traced here: 53.7 us
  Pallas kernels  50.4 us (93%)
  local copies, waits for them, and re-layouts  2.66 us (5%)
  between operations  0.64 us (1%)
    pallas_call x1, Pallas kernels, on_device(): pl.pallas_call(kernel, name='gauss_newton', out_shape=jax.ShapeDtypeStruc...  50.4 us
    reshape x1, local copies, waits for them, and re-layouts, on_device(): out[36:40].reshape(WIDTH)  1.33 us
    transpose x1, local copies, waits for them, and re-layouts, on_device(): out[0:32, 0:COLS]  1.32 us

profile of v8, /device:TPU:6, one launch (start us, length us, event | category | flops | bytes accessed | tf_op | source)
XLA Modules:
  0.0 53.7 jit_solution(12102149358534496459)
XLA Ops:
  0.6 50.4 %gauss_newton.1 = f32[40,128]{1,0:T(8,128)} custom-call(bf16[3,64,4096]{2,1,0:T(8,128)(2,1)} %s_any.1, bf16[3,4096]{1,0:T(4,128)(2,1)} %res_any.1, f32[6,4,1024]{2,1,0:T(4,128)} %mom_any.1, s32[4,1024]{1,0:T(4,128)} %lab_any.1, f32[4,1024]{1,0:T(4,128)} %mis_any.1), custom_call_target="tpu_custom_call" | custom-call | tf_op jit(solution)/shard_map/gauss_newton/pallas_call | solution.py:429
  51.1 1.3 %slice_bitcast_fusion.1 = (f32[512]{0:T(512)}, f32[512]{0:T(512)}) fusion(f32[40,128]{1,0:T(8,128)} %gauss_newton.1), kind=kLoop, calls=%fused_computation.1 | loop fusion | bytes 8192 | tf_op jit(solution)/shard_map/reshape | solution.py:463
  52.4 1.3 %slice_bitcast_fusion = f32[64,32]{0,1:T(8,128)} fusion(f32[40,128]{1,0:T(8,128)} %gauss_newton.1), kind=kLoop, calls=%fused_computation | loop fusion | bytes 16384 | tf_op jit(solution)/shard_map/transpose | solution.py:463
